TPU v7x, 32 devices: a whole 2x2x4 slice. The times are simulated.
32 devices in a mesh: dp: 8 (over y, x, core), tensor: 4 (over z).
Axes of the slice: x: 2, y: 2, z: 4, core: 2. Of those that a mesh axis runs over, the one named last changes fastest.
Arguments:
- block_input: bfloat16 [2048, 2048], P('dp'), may hold values from -6 to 6
- segment_ids: int32 [8, 256], P('dp'), may hold values from 0 to 2, never falling along the last dimension, each value on 1 to 192 neighbouring positions
- expert_ids: int32 [2048, 8], P('dp'), may hold values from 0 to 31, all different within a row; in each aligned block of 256 rows (0 to 255, 256 to 511, ...) at most 128 rows name the same one
- attn_gain: float32 [2048], replicated, may hold values from 0.25 to 1.75
- query_weight: bfloat16 [2048, 4096], P(None, 'tensor'), may hold values from -0.125 to 0.125
- key_projection: bfloat16 [2048, 512], P(None, 'tensor'), may hold values from -0.125 to 0.125
- value_projection: bfloat16 [2048, 512], P(None, 'tensor'), may hold values from -0.125 to 0.125
- query_norm_gain: float32 [128], replicated, may hold values from 0.25 to 1.75
- key_norm_gain: float32 [128], replicated, may hold values from 0.25 to 1.75
- output_projection: bfloat16 [2048, 4096], P(None, 'tensor'), may hold values from -0.375 to 0.375
- ffn_gain: float32 [2048], replicated, may hold values from 0.25 to 1.75
- router_weight: bfloat16 [2048, 32], replicated, may hold values from -0.0625 to 0.0625
- gate_experts: bfloat16 [32, 2048, 768], P('dp', None, 'tensor'), may hold values from -0.125 to 0.125
- up_experts: bfloat16 [32, 2048, 768], P('dp', None, 'tensor'), may hold values from -0.125 to 0.125
- down_experts: bfloat16 [32, 768, 2048], P('dp', 'tensor'), may hold values from -0.4375 to 0.4375
- out_grad: bfloat16 [2048, 2048], P('dp'), may hold values from -6 to 6
Outputs:
- block_output: bfloat16 [2048, 2048], P('dp')
- input_grad: bfloat16 [2048, 2048], P('dp')
- attn_gain_grad: float32 [2048], P('dp')
- query_weight_grad: float32 [2048, 4096], P('dp', 'tensor')
- key_weight_grad: float32 [2048, 512], P('dp', 'tensor')
- value_weight_grad: float32 [2048, 512], P('dp', 'tensor')
- query_gain_grad: float32 [128], P('dp')
- key_gain_grad: float32 [128], P('dp')
- out_weight_grad: float32 [2048, 4096], P('dp', 'tensor')
- ffn_gain_grad: float32 [2048], P('dp')
- router_weight_grad: float32 [2048, 32], P('dp')
- gate_experts_grad: float32 [32, 2048, 768], P('dp', None, 'tensor')
- up_experts_grad: float32 [32, 2048, 768], P('dp', None, 'tensor')
- down_experts_grad: float32 [32, 768, 2048], P('dp', 'tensor')
Inputs may be any that keep to these rules, and one draw needn't show every extreme that they name: `segment_ids`: segment ids never fall along a row; each segment holds 1 to 192 tokens and one of each row holds exactly 192. `expert_ids`: each row names 8 different experts. No expert is named by more than 128 of the rows of one index of dp, a bound that some block reaches by the rows of some index of dp.
All inputs are finite; a program needn't handle non-finite values.
Results may differ from a plain program's by a relative error of at most 0.03.
Values may be sent and summed in bfloat16 or wider, within the bound.
No kernel may reach another device: no remote copies, remote signals or barrier semaphores. Data moves between devices by JAX's collectives and lax.ppermute only.
A program may use at most 320 MiB of HBM per device.

v0:
```python
import jax
import jax.numpy as jnp
from jax import lax
from jax.sharding import PartitionSpec as P

EPS = 1e-06
THETA = 1000000.0
BLOCK_ROWS = 512


def rms_scale(value_tensor):
    return lax.rsqrt(jnp.mean(value_tensor * value_tensor, axis=-1, keepdims=True) + EPS)


def norm_reverse(grad_rows, normed, scale_rows):
    return scale_rows * (grad_rows - normed * jnp.mean(grad_rows * normed, axis=-1, keepdims=True))


def rope_tables(segment_row, head_dim):
    row_count = segment_row.shape[0]
    index_row = jnp.arange(row_count, dtype=jnp.int32)
    same_seg = segment_row[:, None] == segment_row[None, :]
    before = index_row[None, :] < index_row[:, None]
    positions = jnp.sum((same_seg & before).astype(jnp.int32), axis=1)
    half_dim = head_dim // 2
    frequency = THETA ** (-(jnp.arange(half_dim, dtype=jnp.float32) * 2.0) / head_dim)
    angles = positions.astype(jnp.float32)[:, None] * frequency[None, :]
    return (jnp.cos(angles), jnp.sin(angles))


def apply_rotation(value_tensor, cosine_table, sine_lookup):
    half_dim = value_tensor.shape[-1] // 2
    low_half = value_tensor[..., :half_dim]
    high_half = value_tensor[..., half_dim:]
    cos_rows = cosine_table[:, None, :]
    sin_rows = sine_lookup[:, None, :]
    return jnp.concatenate(
        [low_half * cos_rows - high_half * sin_rows, high_half * cos_rows + low_half * sin_rows],
        axis=-1,
    )


def rotate_back(grad_rows, cosine_table, sine_lookup):
    half_dim = grad_rows.shape[-1] // 2
    low_half = grad_rows[..., :half_dim]
    high_half = grad_rows[..., half_dim:]
    cos_rows = cosine_table[:, None, :]
    sin_rows = sine_lookup[:, None, :]
    return jnp.concatenate(
        [low_half * cos_rows + high_half * sin_rows, high_half * cos_rows - low_half * sin_rows],
        axis=-1,
    )


def score_block(block_start, block_rows, query_rotated, key_rot, segment_row, scale_value):
    query_pos = block_start + jnp.arange(block_rows, dtype=jnp.int32)
    key_pos = jnp.arange(segment_row.shape[0], dtype=jnp.int32)
    allowed = (segment_row[:, None] == segment_row[None, :]) & (
        key_pos[None, :] <= query_pos[:, None]
    )
    scores = (
        jnp.einsum("qkgd,skd->kgqs", query_rotated, key_rot, preferred_element_type=jnp.float32)
        * scale_value
    )
    return (query_rotated, jnp.where(allowed, scores, -jnp.inf))


def attend_forward(query_rotated, key_rot, value_row_block, segment_row, scale_value):
    total_rows = query_rotated.shape[0]
    blocks = max(1, total_rows // BLOCK_ROWS)
    block_rows = total_rows // blocks

    def one_block(block_index):
        query_block, scores = score_block(
            block_index * block_rows, block_rows, query_rotated, key_rot, segment_row, scale_value
        )
        top_score = jnp.max(scores, axis=-1, keepdims=True)
        weights = jnp.exp(scores - top_score)
        totals = jnp.sum(weights, axis=-1, keepdims=True)
        prob_rows = (weights / totals).astype(jnp.bfloat16)
        mixed_rows = jnp.einsum(
            "kgqs,skd->qkgd", prob_rows, value_row_block, preferred_element_type=jnp.float32
        )
        return (mixed_rows.astype(jnp.bfloat16), top_score + jnp.log(totals))

    outputs, log_sums = lax.map(one_block, jnp.arange(blocks, dtype=jnp.int32))
    return (outputs.reshape((total_rows,) + outputs.shape[2:]), log_sums)


def attend_backward(
    query_rotated,
    key_rot,
    value_row_block,
    segment_row,
    attn_out,
    attention_output_gradient,
    log_sums,
    scale_value,
):
    total_rows = query_rotated.shape[0]
    blocks = max(1, total_rows // BLOCK_ROWS)
    block_rows = total_rows // blocks

    def one_block(carry, block_index):
        key_acc, value_acc = carry
        block_start = block_index * block_rows
        query_block, scores = score_block(
            block_start, block_rows, query_rotated, key_rot, segment_row, scale_value
        )
        prob_full = jnp.exp(scores - log_sums[block_index])
        prob_half = prob_full.astype(jnp.bfloat16)
        row_delta = jnp.sum(
            attention_output_gradient.astype(jnp.float32) * attn_out.astype(jnp.float32), axis=-1
        )
        row_delta = jnp.transpose(row_delta, (1, 2, 0))[..., None]
        value_acc = value_acc + jnp.einsum(
            "kgqs,qkgd->skd",
            prob_half,
            attention_output_gradient,
            preferred_element_type=jnp.float32,
        )
        prob_grad = jnp.einsum(
            "qkgd,skd->kgqs",
            attention_output_gradient,
            value_row_block,
            preferred_element_type=jnp.float32,
        )
        score_grad = (prob_full * (prob_grad - row_delta) * scale_value).astype(jnp.bfloat16)
        query_grad = jnp.einsum(
            "kgqs,skd->qkgd", score_grad, key_rot, preferred_element_type=jnp.float32
        )
        key_acc = key_acc + jnp.einsum(
            "kgqs,qkgd->skd", score_grad, query_block, preferred_element_type=jnp.float32
        )
        return ((key_acc, value_acc), query_grad)

    zero_keys = jnp.zeros(key_rot.shape, jnp.float32)
    (key_grad, value_gradient), query_grads = lax.scan(
        one_block, (zero_keys, zero_keys), jnp.arange(blocks, dtype=jnp.int32)
    )
    return (query_grads.reshape(query_rotated.shape), key_grad, value_gradient)


def pick_slots(token_rows, slot_token, slot_weight):
    is_valid = slot_token >= 0
    picked = jnp.take(token_rows, jnp.maximum(slot_token, 0), axis=0)
    if slot_weight is None:
        return jnp.where(is_valid[:, None], picked, jnp.zeros((), picked.dtype))
    scaled = picked.astype(jnp.float32) * slot_weight[:, None]
    return scaled.astype(jnp.bfloat16)


def dispatch(token_rows, slot_token, slot_weight, experts_dev, capacity):
    data_count = lax.axis_size("dp")
    picked = pick_slots(token_rows, slot_token, slot_weight)
    buffer = picked.reshape(data_count, experts_dev, capacity, picked.shape[1])
    return lax.all_to_all(buffer, "dp", split_axis=0, concat_axis=0, tiled=True)


def local(
    block_input,
    segment_ids,
    expert_ids,
    attn_gain,
    query_weight,
    key_projection,
    value_projection,
    query_norm_gain,
    key_norm_gain,
    output_projection,
    ffn_gain,
    router_weight,
    gate_experts,
    up_experts,
    down_experts,
    out_grad,
):
    tokens_dev = block_input.shape[0]
    model_width = block_input.shape[1]
    head_dim = query_norm_gain.shape[0]
    top_count = expert_ids.shape[1]
    experts_dev = gate_experts.shape[0]
    num_experts = experts_dev * lax.axis_size("dp")
    capacity = tokens_dev * top_count * 2 // num_experts
    tensor_count = lax.axis_size("tensor")
    quarter = model_width // tensor_count
    col_start = lax.axis_index("tensor") * quarter
    scale_value = head_dim ** (-0.5)
    segment_row = segment_ids[0]
    inputs_f = block_input.astype(jnp.float32)
    scale_one = rms_scale(inputs_f)
    normed_one = inputs_f * scale_one
    attention_input = (normed_one * attn_gain).astype(jnp.bfloat16)
    cosine_table, sine_lookup = rope_tables(segment_row, head_dim)
    query_raw = jnp.dot(attention_input, query_weight, preferred_element_type=jnp.float32).reshape(
        tokens_dev, -1, head_dim
    )
    query_scale = rms_scale(query_raw)
    query_normalized = query_raw * query_scale
    key_unnormed = jnp.dot(
        attention_input, key_projection, preferred_element_type=jnp.float32
    ).reshape(tokens_dev, -1, head_dim)
    key_norm_scale = rms_scale(key_unnormed)
    key_normalized = key_unnormed * key_norm_scale
    key_rot = apply_rotation(key_normalized * key_norm_gain, cosine_table, sine_lookup).astype(
        jnp.bfloat16
    )
    value_row_block = (
        jnp.dot(attention_input, value_projection, preferred_element_type=jnp.float32)
        .astype(jnp.bfloat16)
        .reshape(tokens_dev, -1, head_dim)
    )
    local_heads = query_raw.shape[1]
    local_kv = key_unnormed.shape[1]
    group_width = local_heads // local_kv
    query_rotated = (
        apply_rotation(query_normalized * query_norm_gain, cosine_table, sine_lookup)
        .astype(jnp.bfloat16)
        .reshape(tokens_dev, local_kv, group_width, head_dim)
    )
    attn_out, log_sums = attend_forward(
        query_rotated, key_rot, value_row_block, segment_row, scale_value
    )
    attn_flat = attn_out.reshape(tokens_dev, local_heads * head_dim)
    attn_part = lax.dot_general(
        attn_flat, output_projection, (((1,), (1,)), ((), ())), preferred_element_type=jnp.float32
    )
    attn_total = lax.psum(attn_part.astype(jnp.bfloat16), "tensor").astype(jnp.float32)
    middle = inputs_f + attn_total
    scale_two = rms_scale(middle)
    normed_two = middle * scale_two
    ffn_in = (normed_two * ffn_gain).astype(jnp.bfloat16)
    logits = jnp.dot(ffn_in, router_weight, preferred_element_type=jnp.float32)
    logit_exp = jnp.exp(logits - jnp.max(logits, axis=-1, keepdims=True))
    router_prob = logit_exp / jnp.sum(logit_exp, axis=-1, keepdims=True)
    choose_hot = expert_ids[:, :, None] == jnp.arange(num_experts, dtype=jnp.int32)[None, None, :]
    choose_int = choose_hot.astype(jnp.int32)
    choose_float = choose_hot.astype(jnp.float32)
    selected = jnp.sum(choose_float * router_prob[:, None, :], axis=2)
    select_total = jnp.sum(selected, axis=-1, keepdims=True)
    gate_values = selected / select_total
    member = jnp.sum(choose_int, axis=1)
    earlier = jnp.cumsum(member, axis=0) - member
    slot_pos = jnp.sum(choose_int * earlier[:, None, :], axis=2)
    slot_index = expert_ids * capacity + slot_pos
    flat_slots = slot_index.reshape(-1)
    token_index = jnp.repeat(jnp.arange(tokens_dev, dtype=jnp.int32), top_count)
    slot_token = jnp.full((num_experts * capacity,), -1, jnp.int32).at[flat_slots].set(token_index)
    slot_gate = (
        jnp.zeros((num_experts * capacity,), jnp.float32)
        .at[flat_slots]
        .set(gate_values.reshape(-1))
    )
    received = dispatch(ffn_in, slot_token, None, experts_dev, capacity)
    gate_pre = jnp.einsum(
        "secd,edf->secf", received, gate_experts, preferred_element_type=jnp.float32
    )
    up_pre = jnp.einsum("secd,edf->secf", received, up_experts, preferred_element_type=jnp.float32)
    activated = jax.nn.silu(gate_pre)
    hidden = (activated * up_pre).astype(jnp.bfloat16)
    partial_out = jnp.einsum(
        "secf,efd->secd", hidden, down_experts, preferred_element_type=jnp.float32
    )
    expert_out = lax.psum_scatter(
        partial_out.astype(jnp.bfloat16), "tensor", scatter_dimension=3, tiled=True
    )
    returned = lax.all_to_all(expert_out, "dp", split_axis=0, concat_axis=0, tiled=True).reshape(
        num_experts * capacity, quarter
    )
    slot_values = (
        jnp.take(returned, flat_slots, axis=0)
        .reshape(tokens_dev, top_count, quarter)
        .astype(jnp.float32)
    )
    mix_part = jnp.sum(gate_values[:, :, None] * slot_values, axis=1)
    middle_part = lax.dynamic_slice_in_dim(middle, col_start, quarter, 1)
    out_part = (middle_part + mix_part).astype(jnp.bfloat16)
    block_output = lax.all_gather(out_part, "tensor", axis=1, tiled=True)
    grad_f = out_grad.astype(jnp.float32)
    grad_quarter = lax.dynamic_slice_in_dim(grad_f, col_start, quarter, 1)
    gate_grad_part = jnp.sum(grad_quarter[:, None, :] * slot_values, axis=-1)
    grad_recv = dispatch(out_grad, slot_token, slot_gate, experts_dev, capacity)
    hidden_grad = jnp.einsum(
        "secd,efd->secf", grad_recv, down_experts, preferred_element_type=jnp.float32
    )
    sigmoid_gate = jax.nn.sigmoid(gate_pre)
    gate_pre_grad = (
        hidden_grad * up_pre * sigmoid_gate * (1.0 + gate_pre * (1.0 - sigmoid_gate))
    ).astype(jnp.bfloat16)
    up_pre_grad = (hidden_grad * activated).astype(jnp.bfloat16)
    down_experts_grad = jnp.einsum(
        "secf,secd->efd", hidden, grad_recv, preferred_element_type=jnp.float32
    )
    gate_experts_grad = jnp.einsum(
        "secd,secf->edf", received, gate_pre_grad, preferred_element_type=jnp.float32
    )
    up_experts_grad = jnp.einsum(
        "secd,secf->edf", received, up_pre_grad, preferred_element_type=jnp.float32
    )
    input_part = jnp.einsum(
        "secf,edf->secd", gate_pre_grad, gate_experts, preferred_element_type=jnp.float32
    ) + jnp.einsum("secf,edf->secd", up_pre_grad, up_experts, preferred_element_type=jnp.float32)
    slot_back = lax.psum_scatter(
        input_part.astype(jnp.bfloat16), "tensor", scatter_dimension=3, tiled=True
    )
    back_rows = lax.all_to_all(slot_back, "dp", split_axis=0, concat_axis=0, tiled=True).reshape(
        num_experts * capacity, quarter
    )
    back_taken = jnp.take(back_rows, flat_slots, axis=0).reshape(tokens_dev, top_count, quarter)
    ffn_back_part = jnp.sum(back_taken.astype(jnp.float32), axis=1)
    ffn_back, gate_parts = (
        lax.all_gather(ffn_back_part.astype(jnp.bfloat16), "tensor", axis=1, tiled=True).astype(
            ffn_back_part.dtype
        ),
        lax.all_gather(gate_grad_part.astype(jnp.bfloat16), "tensor", axis=1, tiled=True).astype(
            gate_grad_part.dtype
        ),
    )
    gate_grad = jnp.sum(gate_parts.reshape(tokens_dev, tensor_count, top_count), axis=1)
    select_grad = (
        gate_grad - jnp.sum(gate_grad * gate_values, axis=-1, keepdims=True)
    ) / select_total
    prob_grad = jnp.sum(choose_float * select_grad[:, :, None], axis=1)
    logit_grad = (
        router_prob * (prob_grad - jnp.sum(prob_grad * router_prob, axis=-1, keepdims=True))
    ).astype(jnp.bfloat16)
    router_part = lax.dot_general(
        ffn_in, logit_grad, (((0,), (0,)), ((), ())), preferred_element_type=jnp.float32
    )
    ffn_grad = ffn_back + lax.dot_general(
        logit_grad, router_weight, (((1,), (1,)), ((), ())), preferred_element_type=jnp.float32
    )
    ffn_gain_part = jnp.sum(ffn_grad * normed_two, axis=0)
    mid_grad = grad_f + norm_reverse(ffn_grad * ffn_gain, normed_two, scale_two)
    middle_gradient_second = mid_grad.astype(jnp.bfloat16)
    out_weight_part = lax.dot_general(
        middle_gradient_second,
        attn_flat,
        (((0,), (0,)), ((), ())),
        preferred_element_type=jnp.float32,
    )
    attention_output_gradient = jnp.dot(
        middle_gradient_second, output_projection, preferred_element_type=jnp.float32
    ).astype(jnp.bfloat16)
    attention_output_gradient = lax.optimization_barrier(attention_output_gradient).reshape(
        tokens_dev, local_kv, group_width, head_dim
    )
    query_grad, key_grad, value_gradient = attend_backward(
        query_rotated,
        key_rot,
        value_row_block,
        segment_row,
        attn_out,
        attention_output_gradient,
        log_sums,
        scale_value,
    )
    query_back = rotate_back(
        query_grad.reshape(tokens_dev, local_heads, head_dim), cosine_table, sine_lookup
    )
    query_gain_part = jnp.sum(query_back * query_normalized, axis=(0, 1))
    query_raw_grad = (
        norm_reverse(query_back * query_norm_gain, query_normalized, query_scale)
        .astype(jnp.bfloat16)
        .reshape(tokens_dev, -1)
    )
    key_reverse = rotate_back(key_grad, cosine_table, sine_lookup)
    key_gain_part = jnp.sum(key_reverse * key_normalized, axis=(0, 1))
    key_unnormed_gradient = (
        norm_reverse(key_reverse * key_norm_gain, key_normalized, key_norm_scale)
        .astype(jnp.bfloat16)
        .reshape(tokens_dev, -1)
    )
    value_gradient_second = value_gradient.astype(jnp.bfloat16).reshape(tokens_dev, -1)
    contract_rows = (((0,), (0,)), ((), ()))
    contract_cols = (((1,), (1,)), ((), ()))
    query_part = lax.dot_general(
        attention_input, query_raw_grad, contract_rows, preferred_element_type=jnp.float32
    )
    key_part = lax.dot_general(
        attention_input, key_unnormed_gradient, contract_rows, preferred_element_type=jnp.float32
    )
    value_part = lax.dot_general(
        attention_input, value_gradient_second, contract_rows, preferred_element_type=jnp.float32
    )
    attn_in_part = (
        lax.dot_general(
            query_raw_grad, query_weight, contract_cols, preferred_element_type=jnp.float32
        )
        + lax.dot_general(
            key_unnormed_gradient, key_projection, contract_cols, preferred_element_type=jnp.float32
        )
        + lax.dot_general(
            value_gradient_second,
            value_projection,
            contract_cols,
            preferred_element_type=jnp.float32,
        )
    )
    attn_in_grad, query_gain_sum, key_gain_sum = (
        lax.psum(attn_in_part.astype(jnp.bfloat16), "tensor").astype(jnp.float32),
        lax.psum(query_gain_part.astype(jnp.bfloat16), "tensor").astype(jnp.float32),
        lax.psum(key_gain_part.astype(jnp.bfloat16), "tensor").astype(jnp.float32),
    )
    attn_gain_part = jnp.sum(attn_in_grad * normed_one, axis=0)
    input_grad = (mid_grad + norm_reverse(attn_in_grad * attn_gain, normed_one, scale_one)).astype(
        jnp.bfloat16
    )
    (
        query_weight_grad,
        key_weight_grad,
        value_weight_grad,
        out_weight_grad,
        router_weight_grad,
        attn_gain_grad,
        ffn_gain_grad,
        query_gain_grad,
        key_gain_grad,
    ) = (
        lax.psum_scatter(
            query_part.astype(jnp.bfloat16), "dp", scatter_dimension=0, tiled=True
        ).astype(jnp.float32),
        lax.psum_scatter(
            key_part.astype(jnp.bfloat16), "dp", scatter_dimension=0, tiled=True
        ).astype(jnp.float32),
        lax.psum_scatter(
            value_part.astype(jnp.bfloat16), "dp", scatter_dimension=0, tiled=True
        ).astype(jnp.float32),
        lax.psum_scatter(
            out_weight_part.astype(jnp.bfloat16), "dp", scatter_dimension=0, tiled=True
        ).astype(jnp.float32),
        lax.psum_scatter(
            router_part.astype(jnp.bfloat16), "dp", scatter_dimension=0, tiled=True
        ).astype(jnp.float32),
        lax.psum_scatter(
            attn_gain_part.astype(jnp.bfloat16), "dp", scatter_dimension=0, tiled=True
        ).astype(jnp.float32),
        lax.psum_scatter(
            ffn_gain_part.astype(jnp.bfloat16), "dp", scatter_dimension=0, tiled=True
        ).astype(jnp.float32),
        lax.psum_scatter(
            query_gain_sum.astype(jnp.bfloat16), "dp", scatter_dimension=0, tiled=True
        ).astype(jnp.float32),
        lax.psum_scatter(
            key_gain_sum.astype(jnp.bfloat16), "dp", scatter_dimension=0, tiled=True
        ).astype(jnp.float32),
    )
    return (
        block_output,
        input_grad,
        attn_gain_grad,
        query_weight_grad,
        key_weight_grad,
        value_weight_grad,
        query_gain_grad,
        key_gain_grad,
        out_weight_grad,
        ffn_gain_grad,
        router_weight_grad,
        gate_experts_grad,
        up_experts_grad,
        down_experts_grad,
    )


def solution(mesh):
    return jax.shard_map(
        local,
        mesh=mesh,
        in_specs=(
            P("dp", None),
            P("dp", None),
            P("dp", None),
            P(),
            P(None, "tensor"),
            P(None, "tensor"),
            P(None, "tensor"),
            P(),
            P(),
            P(None, "tensor"),
            P(),
            P(),
            P("dp", None, "tensor"),
            P("dp", None, "tensor"),
            P("dp", "tensor", None),
            P("dp", None),
        ),
        out_specs=(
            P("dp", None),
            P("dp", None),
            P("dp"),
            P("dp", "tensor"),
            P("dp", "tensor"),
            P("dp", "tensor"),
            P("dp"),
            P("dp"),
            P("dp", "tensor"),
            P("dp"),
            P("dp", None),
            P("dp", None, "tensor"),
            P("dp", None, "tensor"),
            P("dp", "tensor", None),
        ),
        check_vma=False,
    )
```

profile of v0, /device:TPU:0, one launch (start us, length us, event | category | flops | bytes accessed | tf_op | source)
XLA Modules:
  0.0 1653.1 jit_solution(10588273651753471017)
XLA Ops:
  29.3 8.1 scatter_custom_fusion
  37.4 45.2 %all-reduce.9.cloned.1.call-done = bf16[256,2048]{1,0:T(8,128)(2,1)} async-done(((bf16[256,2048]{1,0:T(8,128)(2,1)}), bf16[256,2048]{1,0:T(8,128)(2,1)}) %all-reduce.9.cloned.1.call-update) | async-done | bytes 1048592 | tf_op jit(solution)/shard_map/psum | solution.py:228
  86.2 32.7 %gather_fusion = bf16[4096,2048]{1,0:T(8,128)(2,1)} fusion(bf16[256,2048]{1,0:T(8,128)(2,1)} %multiply_convert_fusion.1, s32[4096]{0:T(1024)S(1)} %maximum_clamp_fusion), kind=kCustom, calls=%fused_computation.clone | custom fusion | bytes 33570816 | tf_op jit(solution)/shard_map/jit(_take)/gather | solution.py:146
  118.9 9.5 select_select_fusion
  128.4 188.4 %all_to_all.20 = bf16[8,4,128,2048]{3,2,1,0:T(8,128)(2,1)} all-to-all(bf16[8,4,128,2048]{3,2,1,0:T(8,128)(2,1)S(1)} %bitcast.280), channel_id=1, replica_groups=mesh['dp'=8,'tensor'=4] {'dp'}, dimensions={0} | all-to-all | bytes 33554432 | tf_op jit(solution)/shard_map/all_to_all | solution.py:157
  316.8 9.4 fusion.6
  326.2 12.1 fusion.26
  338.3 9.6 convert_bitcast_fusion
  347.9 278.1 %reduce-scatter.8.cloned.1.call-done = bf16[8,4,128,512]{3,2,0,1:T(8,128)(2,1)} async-done(((bf16[8,4,128,2048]{3,2,0,1:T(8,128)(2,1)}), bf16[8,4,128,512]{3,2,0,1:T(8,128)(2,1)}) %reduce-scatter.8.cloned.1.call-update) | async-done | bytes 4194320 | tf_op jit(solution)/shard_map/reduce_scatter | solution.py:264
  638.2 32.7 %gather_fusion.2 = bf16[4096,2048]{1,0:T(8,128)(2,1)} fusion(bf16[256,2048]{1,0:T(8,128)(2,1)} %param.35, s32[4096]{0:T(1024)S(1)} %maximum_clamp_fusion), kind=kCustom, calls=%fused_computation.2.clone | custom fusion | bytes 33570816 | tf_op jit(solution)/shard_map/jit(_take)/gather | solution.py:146
  675.1 9.1 all-to-all-done.1
  684.3 12.0 gather_fusion.1
  698.8 14.1 all_gather.11
  713.1 8.2 scatter_custom_fusion.1
  721.3 10.0 multiply_convert_fusion
  731.4 187.6 %all_to_all.21 = bf16[8,4,128,2048]{3,2,1,0:T(8,128)(2,1)} all-to-all(bf16[8,4,128,2048]{3,2,1,0:T(8,128)(2,1)S(1)} %bitcast.281), channel_id=1, replica_groups=mesh['dp'=8,'tensor'=4] {'dp'}, dimensions={0} | all-to-all | bytes 33554432 | tf_op jit(solution)/shard_map/all_to_all | solution.py:157
  919.0 10.8 fusion.23
  929.8 16.3 fusion.17
  946.1 16.8 %fusion.8 = bf16[8,4,128,2048]{3,2,0,1:T(8,128)(2,1)} fusion(f32[4,8,128,2048]{3,2,1,0:T(8,128)} %fusion.17, bf16[8,4,128,192]{2,3,0,1:T(8,128)(2,1)S(1)} %get-tuple-element.86, bf16[4,2048,192]{1,2,0:T(8,128)(2,1)S(1)} %copy-done.26), kind=kOutput, calls=%fused_computation.18 | convolution fusion | flops 3238002688 | bytes 55050240 | tf_op jit(solution)/shard_map/secf,edf->secd/dot_general | solution.py:302
  963.0 278.4 %reduce-scatter.10.cloned.1.call-done = bf16[8,4,128,512]{3,2,0,1:T(8,128)(2,1)} async-done(((bf16[8,4,128,2048]{3,2,0,1:T(8,128)(2,1)}), bf16[8,4,128,512]{3,2,0,1:T(8,128)(2,1)}) %reduce-scatter.10.cloned.1.call-update) | async-done | bytes 4194320 | tf_op jit(solution)/shard_map/reduce_scatter | solution.py:303
  1244.0 52.6 %all_to_all.22 = bf16[8,4,128,512]{3,2,1,0:T(8,128)(2,1)} all-to-all(bf16[8,4,128,512]{3,2,1,0:T(8,128)(2,1)S(1)} %copy.188), channel_id=1, replica_groups=mesh['dp'=8,'tensor'=4] {'dp'}, dimensions={0} | all-to-all | bytes 8388608 | tf_op jit(solution)/shard_map/all_to_all | solution.py:306
  1296.6 12.0 gather_fusion.3
  1322.3 17.3 %all-gather.5.cloned.1.call-done = bf16[256,2048]{1,0:T(8,128)(2,1)} async-done(((bf16[256,512]{1,0:T(8,128)(2,1)}), bf16[256,2048]{1,0:T(8,128)(2,1)}) %all-gather.5.cloned.1.call-update) | async-done | bytes 1048592 | tf_op jit(solution)/shard_map/all_gather | solution.py:312
  1401.9 9.9 fusion.12
  1411.8 10.3 convolution_bitcast_fusion
  1430.5 37.5 %all-reduce.11.cloned.1.call-done = bf16[256,2048]{1,0:T(8,128)(2,1)} async-done(((bf16[256,2048]{1,0:T(8,128)(2,1)}), bf16[256,2048]{1,0:T(8,128)(2,1)}) %all-reduce.11.cloned.1.call-update) | async-done | bytes 1048592 | tf_op jit(solution)/shard_map/psum | solution.py:401
  1470.4 14.2 all-reduce.4
  1484.8 20.3 %reduce-scatter.14.cloned.1.call-done = bf16[256,128]{1,0:T(8,128)(2,1)} async-done(((bf16[2048,128]{1,0:T(8,128)(2,1)}), bf16[256,128]{1,0:T(8,128)(2,1)}) %reduce-scatter.14.cloned.1.call-update) | async-done | bytes 65552 | tf_op jit(solution)/shard_map/reduce_scatter | solution.py:423
  1506.6 11.9 all-reduce.5
  1523.9 10.8 all-gather.3.cloned.1.call-done
  1534.7 53.7 %reduce-scatter.18.cloned.1.call-done = bf16[256,1024]{1,0:T(8,128)(2,1)} async-done(((bf16[2048,1024]{1,0:T(8,128)(2,1)}), bf16[256,1024]{1,0:T(8,128)(2,1)}) %reduce-scatter.18.cloned.1.call-update) | async-done | bytes 524304 | tf_op jit(solution)/shard_map/reduce_scatter | solution.py:429
  1590.5 52.4 %reduce-scatter.12.cloned.1.call-done = bf16[256,1024]{1,0:T(8,128)(2,1)} async-done(((bf16[2048,1024]{1,0:T(8,128)(2,1)}), bf16[256,1024]{1,0:T(8,128)(2,1)}) %reduce-scatter.12.cloned.1.call-update) | async-done | bytes 524304 | tf_op jit(solution)/shard_map/reduce_scatter | solution.py:420
  (341 shorter events, 144.5 us)
Async XLA Ops:
  7.2 331.2 %copy-start = (bf16[4,192,2048]{2,1,0:T(8,128)(2,1)S(1)}, bf16[4,192,2048]{2,1,0:T(8,128)(2,1)}, u32[]{:S(2)}) copy-start(bf16[4,192,2048]{2,1,0:T(8,128)(2,1)} %param.34) | copy-start | bytes 9437188
  7.2 75.4 %all-reduce.9.cloned.1.call-start = ((), (), s32[]{:S(2)}) async-start(), calls=%async_computation.11 | async-start | bytes 2097152 | tf_op jit(solution)/shard_map/psum | solution.py:228
  27.8 56.9 %copy-start.62 = (f32[2048]{0:T(1024)S(1)}, f32[2048]{0:T(1024)}, u32[]{:S(2)}) copy-start(f32[2048]{0:T(1024)} %param.30) | copy-start | bytes 24580
  27.8 598.2 %reduce-scatter.8.cloned.1.call-start = ((), (), s32[]{:S(2)}) async-start(), calls=%async_computation.12 | async-start | bytes 20971520 | tf_op jit(solution)/shard_map/reduce_scatter | solution.py:264
  84.8 34.2 %copy-start.75 = (f32[256]{0:T(256)}, f32[256]{0:T(256)S(1)}, u32[]{:S(2)}) copy-start(f32[256]{0:T(256)S(1)} %add_rsqrt_fusion.1) | copy-start | bytes 3076
  128.4 188.4 %copy-start.24 = (bf16[4,2048,192]{1,2,0:T(8,128)(2,1)S(1)}, bf16[4,2048,192]{1,2,0:T(8,128)(2,1)}, u32[]{:S(2)}) copy-start(bf16[4,2048,192]{1,2,0:T(8,128)(2,1)} %param.32) | copy-start | bytes 9437188
  326.2 12.2 copy-start.93
  630.6 53.7 %all-to-all-start.1 = ((bf16[8,4,128,512]{3,2,1,0:T(8,128)(2,1)}), bf16[8,4,128,512]{3,2,1,0:T(8,128)(2,1)}, u32[]{:S(2)}, u32[]{:S(2)}) async-start(bf16[8,4,128,512]{3,2,1,0:T(8,128)(2,1)} %copy.185), calls=%async_computation.2 | async-start | bytes 8388608 | tf_op jit(solution)/shard_map/all_to_all | solution.py:267
  635.2 606.2 %reduce-scatter.10.cloned.1.call-start = ((), (), s32[]{:S(2)}) async-start(), calls=%async_computation.14 | async-start | bytes 20971520 | tf_op jit(solution)/shard_map/reduce_scatter | solution.py:303
  638.2 34.6 %copy-start.55 = (bf16[2048,32]{0,1:T(8,128)(2,1)S(1)}, bf16[2048,32]{0,1:T(8,128)(2,1)}, u32[]{:S(2)}) copy-start(bf16[2048,32]{0,1:T(8,128)(2,1)} %param.31) | copy-start | bytes 393220
  672.7 635.8 %copy-start.64 = (pred[2048]{0:T(1024)(128)(4,1)}, pred[2048]{0:T(1024)(128)(4,1)S(1)}, u32[]{:S(2)}) copy-start(pred[2048]{0:T(1024)(128)(4,1)S(1)} %compare_and_fusion.2) | copy-start | bytes 6148
  675.1 37.7 %copy-start.77 = (f32[256]{0:T(256)}, f32[256]{0:T(256)S(1)}, u32[]{:S(2)}) copy-start(f32[256]{0:T(256)S(1)} %get-tuple-element.76) | copy-start | bytes 3076
  929.8 16.3 copy-start.13
  929.8 16.3 copy-start.15
  929.8 16.3 copy-start.26
  962.9 376.7 %all-gather.5.cloned.1.call-start = ((), (), s32[]{:S(2)}) async-start(), calls=%async_computation.15 | async-start | bytes 1310720 | tf_op jit(solution)/shard_map/all_gather | solution.py:312
  1312.7 87.8 %reduce-scatter.20.cloned.1.call-start = ((), (), s32[]{:S(2)}) async-start(), calls=%async_computation.21 | async-start | bytes 147456 | tf_op jit(solution)/shard_map/reduce_scatter | solution.py:432
  1316.5 23.2 %copy-start.63 = (f32[2048]{0:T(1024)S(1)}, f32[2048]{0:T(1024)}, u32[]{:S(2)}) copy-start(f32[2048]{0:T(1024)} %param.30) | copy-start | bytes 24580
  1316.5 23.2 %copy-start.76 = (f32[256]{0:T(256)S(1)}, f32[256]{0:T(256)}, u32[]{:S(2)}) copy-start(f32[256]{0:T(256)} %copy-done.75) | copy-start | bytes 3076
  1322.1 106.9 %reduce-scatter.16.cloned.1.call-start = ((), (), s32[]{:S(2)}) async-start(), calls=%async_computation.19 | async-start | bytes 589824 | tf_op jit(solution)/shard_map/reduce_scatter | solution.py:426
  1374.2 93.8 %all-reduce.11.cloned.1.call-start = ((), (), s32[]{:S(2)}) async-start(), calls=%async_computation.16 | async-start | bytes 2097152 | tf_op jit(solution)/shard_map/psum | solution.py:401
  1379.4 125.6 %reduce-scatter.14.cloned.1.call-start = ((), (), s32[]{:S(2)}) async-start(), calls=%async_computation.18 | async-start | bytes 589824 | tf_op jit(solution)/shard_map/reduce_scatter | solution.py:423
  1382.1 152.6 %all-gather.3.cloned.1.call-start = ((), (), s32[]{:S(2)}) async-start(), calls=%async_computation.13 | async-start | bytes 1310720 | tf_op jit(solution)/shard_map/all_gather | solution.py:278
  1388.1 200.3 %reduce-scatter.18.cloned.1.call-start = ((), (), s32[]{:S(2)}) async-start(), calls=%async_computation.20 | async-start | bytes 4718592 | tf_op jit(solution)/shard_map/reduce_scatter | solution.py:429
  1393.2 249.8 %reduce-scatter.12.cloned.1.call-start = ((), (), s32[]{:S(2)}) async-start(), calls=%async_computation.17 | async-start | bytes 4718592 | tf_op jit(solution)/shard_map/reduce_scatter | solution.py:420
  1401.9 20.2 %slice-start = ((s8[16777216]{0:T(1024)(128)(4,1)}), s8[4194304]{0:T(1024)(128)(4,1)S(1)}, s32[]{:S(2)}) async-start(s8[16777216]{0:T(1024)(128)(4,1)} %bitcast.277), calls=%async_computation.22 | async-start | bytes 8388608
  1401.9 20.2 %slice-start.1 = ((s8[16777216]{0:T(1024)(128)(4,1)}), s8[4194304]{0:T(1024)(128)(4,1)S(1)}, s32[]{:S(2)}) async-start(s8[16777216]{0:T(1024)(128)(4,1)} %bitcast.277), calls=%async_computation.23 | async-start | bytes 8388608
  1401.9 20.2 %slice-start.2 = ((s8[16777216]{0:T(1024)(128)(4,1)}), s8[4194304]{0:T(1024)(128)(4,1)S(1)}, s32[]{:S(2)}) async-start(s8[16777216]{0:T(1024)(128)(4,1)} %bitcast.277), calls=%async_computation.24 | async-start | bytes 8388608
  1411.8 10.7 slice-start.3
  1411.8 11.6 copy-start.14
  1428.9 41.5 %copy-start.86 = (bf16[2048]{0:T(1024)(128)(2,1)S(1)}, bf16[2048]{0:T(1024)(128)(2,1)}, u32[]{:S(2)}) copy-start(bf16[2048]{0:T(1024)(128)(2,1)} %get-tuple-element.59) | copy-start | bytes 12292
  1428.9 41.5 %copy-start.87 = (bf16[128]{0:T(256)(128)(2,1)S(1)}, bf16[128]{0:T(256)(128)(2,1)}, u32[]{:S(2)}) copy-start(bf16[128]{0:T(256)(128)(2,1)} %get-tuple-element.74) | copy-start | bytes 772
  (78 other events, 241.4 us)
Sparse Core Ops, SparseCore 0:
  27.9 54.6 all-reduce.8
  348.0 277.8 reduce-scatter.7
  963.0 278.2 reduce-scatter.9
  1312.8 26.7 all-gather.4
  1342.5 32.9 reduce-scatter.19
  1379.0 34.1 reduce-scatter.15
  1416.1 51.8 all-reduce.10
  1471.6 33.3 reduce-scatter.13
  1506.6 28.0 all-gather.2
  1537.9 50.4 reduce-scatter.17
  1591.8 51.1 reduce-scatter.11
where the time goes:
time: 1660 us; the launch traced here: 1650 us
  waiting for transfers between devices  803 us (48%)
  blocking collectives  469 us (28%)
  matrix products  144 us (9%)
  local copies, waits for them, and re-layouts  137 us (8%)
  other arithmetic  78.6 us (5%)
  between operations  16.9 us (1%)
    all_to_all x2, blocking collectives, dispatch(): return lax.all_to_all(buffer, 'dp', split_axis=0, concat_axis=0, tiled=True)  376 us
    reduce_scatter x1, waiting for transfers between devices, local(): lax.psum_scatter(input_part.astype(jnp.bfloat16), 'tensor', scatter_dimen...  278 us
    reduce_scatter x1, waiting for transfers between devices, local(): lax.psum_scatter(partial_out.astype(jnp.bfloat16), 'tensor', scatter_dime...  278 us
    gather x2, local copies, waits for them, and re-layouts, pick_slots(): picked = jnp.take(token_rows, jnp.maximum(slot_token, 0), axis=0)  65.4 us
    reduce_scatter x1, waiting for transfers between devices, local(): lax.psum_scatter(out_weight_part.astype(jnp.bfloat16), 'dp', scatter_dime...  53.7 us
    all_to_all x1, blocking collectives, local(): lax.all_to_all(slot_back, 'dp', split_axis=0, concat_axis=0, tiled=True)  52.6 us
    reduce_scatter x1, waiting for transfers between devices, local(): lax.psum_scatter(query_part.astype(jnp.bfloat16), 'dp', scatter_dimension...  52.4 us
    psum x1, waiting for transfers between devices, local(): lax.psum(attn_part.astype(jnp.bfloat16), 'tensor').astype(jnp.float32)  45.2 us
  transfers between devices with their start and end apart: 12, of which 10 were waited for; matrix products, arithmetic and copies ran while one was open for 9% of the time, Pallas kernels for 0%

commit v1 on v0

v1 whole, which is shorter than its diff:
```python
import jax
import jax.numpy as jnp
from jax import lax
from jax.sharding import PartitionSpec as P

EPS = 1e-06
THETA = 1000000.0
F32 = jnp.float32
BF16 = jnp.bfloat16


def rms_scale(values):
    return lax.rsqrt(jnp.mean(values * values, axis=-1, keepdims=True) + EPS)


def norm_reverse(grad_rows, normed, scale_rows):
    return scale_rows * (grad_rows - normed * jnp.mean(grad_rows * normed, axis=-1, keepdims=True))


def dot_nn(a, b):
    return lax.dot_general(a, b, (((1,), (0,)), ((), ())), preferred_element_type=F32)


def dot_nt(a, b):
    return lax.dot_general(a, b, (((1,), (1,)), ((), ())), preferred_element_type=F32)


def dot_tn(a, b):
    return lax.dot_general(a, b, (((0,), (0,)), ((), ())), preferred_element_type=F32)


def swap(value, bit, count):
    return lax.ppermute(value, "dp", [(i, i ^ bit) for i in range(count)])


def shift(value, step, count):
    return lax.ppermute(value, "tensor", [(i, (i + step) % count) for i in range(count)])


def gather_dp(shard, count):
    if count == 8:
        half = shard.shape[0] // 2
        along_x = swap(shard, 2, count)
        along_y = swap(shard, 4, count)
        mate = swap(shard, 1, count)
        diag_lo = swap(along_y[:half], 2, count)
        diag_hi = swap(along_x[half:], 4, count)
        mate_x = swap(along_x, 1, count)
        mate_y = swap(along_y, 1, count)
        diag = jnp.concatenate([diag_lo, diag_hi], 0)
        mate_d = swap(diag, 1, count)
        return [shard, mate, along_x, mate_x, along_y, mate_y, diag, mate_d]
    return [lax.all_gather(shard, "dp", axis=0, tiled=True)]


def add_b(a, b):
    return (a.astype(F32) + b.astype(F32)).astype(BF16)


def scatter_dp(rows, count):
    if count == 8:
        size = rows.shape[0] // count
        half = size // 2
        chunks = [rows[r * size : (r + 1) * size] for r in range(count)]
        pair = {}
        for r in (6, 4, 2, 0):
            pair[r] = add_b(chunks[r], swap(chunks[r + 1], 1, count))
        from_x = swap(pair[6][:half], 2, count)
        from_y = swap(pair[6][half:], 4, count)
        to_y = jnp.concatenate([add_b(pair[4][:half], from_x), pair[4][half:]], 0)
        to_x = jnp.concatenate([pair[2][:half], add_b(pair[2][half:], from_y)], 0)
        got_x = swap(to_x, 2, count)
        got_y = swap(to_y, 4, count)
        return (pair[0].astype(F32) + got_x.astype(F32) + got_y.astype(F32)).astype(BF16)
    return lax.psum_scatter(rows, "dp", scatter_dimension=0, tiled=True)


def gather_z(shard, count):
    if count == 4:
        half = shard.shape[1] // 2
        prev = shift(shard, 1, count)
        after = shift(shard, -1, count)
        far_lo = shift(prev[:, :half], 1, count)
        far_hi = shift(after[:, half:], -1, count)
        far = jnp.concatenate([far_lo, far_hi], 1)
        return jnp.concatenate([shard, after, far, prev], 0)
    return jnp.concatenate([shard] + [shift(shard, -r, count) for r in range(1, count)], 0)


def scatter_z(rows, count):
    size = rows.shape[0] // count
    block = [rows[r * size : (r + 1) * size] for r in range(count)]
    if count == 4:
        half = rows.shape[1] // 2
        lo = shift(block[2][:, :half], 1, count)
        hi = shift(block[2][:, half:], -1, count)
        up = jnp.concatenate([add_b(block[1][:, :half], lo), block[1][:, half:]], 1)
        down = jnp.concatenate([block[3][:, :half], add_b(block[3][:, half:], hi)], 1)
        got_up = shift(up, 1, count)
        got_down = shift(down, -1, count)
        return block[0].astype(F32) + got_up.astype(F32) + got_down.astype(F32)
    total = block[0].astype(F32)
    for r in range(1, count):
        total = total + shift(block[r], r, count).astype(F32)
    return total


def roll_rows(rows, amount):
    return jnp.roll(rows, amount, axis=0)


def rope_apply(values, cos_rows, sin_rows):
    half = values.shape[-1] // 2
    low, high = values[..., :half], values[..., half:]
    c, s = cos_rows[:, None, :], sin_rows[:, None, :]
    return jnp.concatenate([low * c - high * s, high * c + low * s], axis=-1)


def rope_back(values, cos_rows, sin_rows):
    half = values.shape[-1] // 2
    low, high = values[..., :half], values[..., half:]
    c, s = cos_rows[:, None, :], sin_rows[:, None, :]
    return jnp.concatenate([low * c + high * s, high * c - low * s], axis=-1)


def local(
    block_input,
    segment_ids,
    expert_ids,
    attn_gain,
    query_weight,
    key_projection,
    value_projection,
    query_norm_gain,
    key_norm_gain,
    output_projection,
    ffn_gain,
    router_weight,
    gate_experts,
    up_experts,
    down_experts,
    out_grad,
):
    tokens, width = block_input.shape
    head_dim = query_norm_gain.shape[0]
    experts_dev, _, hidden_dev = gate_experts.shape
    n_dp = lax.axis_size("dp")
    n_t = lax.axis_size("tensor")
    num_experts = experts_dev * n_dp
    part = tokens // n_t
    flat = experts_dev * hidden_dev
    t_index = lax.axis_index("tensor")
    d_index = lax.axis_index("dp")
    turn = t_index * part
    scale_value = head_dim ** (-0.5)

    x_rows = roll_rows(block_input, -turn)
    seg = roll_rows(segment_ids[0], -turn)
    ids = roll_rows(expert_ids, -turn)
    dy_rows = roll_rows(out_grad, -turn)
    order = (jnp.arange(tokens, dtype=jnp.int32) + turn) % tokens

    dy_chunks = gather_dp(dy_rows, n_dp)
    ids_all = jnp.concatenate(gather_dp(ids, n_dp), 0)
    dy_all = jnp.concatenate(dy_chunks, 0)

    inputs_f = x_rows.astype(F32)
    scale_one = rms_scale(inputs_f)
    normed_one = inputs_f * scale_one
    attn_in = (normed_one * attn_gain).astype(BF16)

    same = seg[:, None] == seg[None, :]
    earlier = order[None, :] < order[:, None]
    positions = jnp.sum((same & earlier).astype(jnp.int32), axis=1)
    half_dim = head_dim // 2
    frequency = THETA ** (-(jnp.arange(half_dim, dtype=F32) * 2.0) / head_dim)
    angles = positions.astype(F32)[:, None] * frequency[None, :]
    cos_rows, sin_rows = jnp.cos(angles), jnp.sin(angles)
    allowed = same & (order[None, :] <= order[:, None])

    q_raw = dot_nn(attn_in, query_weight).reshape(tokens, -1, head_dim)
    q_scale = rms_scale(q_raw)
    q_hat = q_raw * q_scale
    k_raw = dot_nn(attn_in, key_projection).reshape(tokens, -1, head_dim)
    k_scale = rms_scale(k_raw)
    k_hat = k_raw * k_scale
    k_rot = rope_apply(k_hat * key_norm_gain, cos_rows, sin_rows).astype(BF16)
    v_rows = dot_nn(attn_in, value_projection).astype(BF16).reshape(tokens, -1, head_dim)
    heads = q_raw.shape[1]
    kv = k_raw.shape[1]
    group = heads // kv
    q_rot = rope_apply(q_hat * query_norm_gain, cos_rows, sin_rows).astype(BF16)
    q_rot = q_rot.reshape(tokens, kv, group, head_dim)
    scores = jnp.einsum("qkgd,skd->kgqs", q_rot, k_rot, preferred_element_type=F32) * scale_value
    scores = jnp.where(allowed, scores, -jnp.inf)
    top = jnp.max(scores, axis=-1, keepdims=True)
    weights = jnp.exp(scores - top)
    totals = jnp.sum(weights, axis=-1, keepdims=True)
    probs = weights / totals
    probs_b = probs.astype(BF16)
    attn_out = jnp.einsum("kgqs,skd->qkgd", probs_b, v_rows, preferred_element_type=F32)
    attn_out = attn_out.astype(BF16)
    attn_flat = attn_out.reshape(tokens, heads * head_dim)
    attn_part = dot_nt(attn_flat, output_projection).astype(BF16)
    attn_sum = scatter_z(attn_part, n_t)

    x_own = inputs_f[:part]
    ids_own = ids[:part]
    middle = x_own + attn_sum
    scale_two = rms_scale(middle)
    normed_two = middle * scale_two
    ffn_own = (normed_two * ffn_gain).astype(BF16)
    ffn_rows = gather_z(ffn_own, n_t)
    x_all = jnp.concatenate(gather_dp(ffn_rows, n_dp), 0)

    def router(rows, chosen):
        logits = dot_nn(rows, router_weight)
        raised = jnp.exp(logits - jnp.max(logits, axis=-1, keepdims=True))
        prob = raised / jnp.sum(raised, axis=-1, keepdims=True)
        names = jnp.arange(num_experts, dtype=jnp.int32)
        mask = jnp.any(chosen[:, :, None] == names[None, None, :], axis=1).astype(F32)
        total = jnp.sum(prob * mask, axis=-1, keepdims=True)
        return prob, mask, total, prob * mask / total

    prob_own, mask_own, total_own, gate_own = router(ffn_own, ids_own)
    gate_all = router(x_all, ids_all)[3]

    owner = d_index * experts_dev + jnp.arange(flat, dtype=jnp.int32) // hidden_dev
    names = jnp.arange(num_experts, dtype=jnp.int32)
    place = (names[:, None] == owner[None, :]).astype(F32)
    gate_wide = jnp.dot(gate_all, place, precision=lax.Precision.HIGHEST)

    wg = jnp.transpose(gate_experts, (0, 2, 1)).reshape(flat, width)
    wu = jnp.transpose(up_experts, (0, 2, 1)).reshape(flat, width)
    wd = down_experts.reshape(flat, width)

    d_hidden = dot_nt(dy_all, wd)
    gate_pre = dot_nt(x_all, wg)
    up_pre = dot_nt(x_all, wu)
    sig = jax.nn.sigmoid(gate_pre)
    act = gate_pre * sig
    hidden = act * up_pre
    hidden_g = (hidden * gate_wide).astype(BF16)
    gate_grads = lax.dot_general(
        hidden * d_hidden, place, (((1,), (1,)), ((), ())), precision=lax.Precision.HIGHEST
    )
    hidden_grad = d_hidden * gate_wide
    dg = (hidden_grad * up_pre * sig * (1.0 + gate_pre * (1.0 - sig))).astype(BF16)
    du = (hidden_grad * act).astype(BF16)
    back = (dot_nn(dg, wg) + dot_nn(du, wu)).astype(BF16)
    pad = (-num_experts) % 128
    back = jnp.concatenate([back, jnp.pad(gate_grads, ((0, 0), (0, pad))).astype(BF16)], 1)
    back_sum = scatter_dp(back, n_dp)
    back_own = scatter_z(back_sum, n_t)
    ffn_back = back_own[:, :width]
    gate_grad = back_own[:, width : width + num_experts]

    mix = dot_nn(hidden_g, wd).astype(BF16)
    mix_sum = scatter_dp(mix, n_dp)
    mix_own = scatter_z(mix_sum, n_t)
    block_out = gather_z((middle + mix_own).astype(BF16), n_t)
    block_output = roll_rows(block_out, turn)

    down_grad = dot_tn(hidden_g, dy_all).reshape(experts_dev, hidden_dev, width)
    gate_w_grad = dot_tn(dg, x_all).reshape(experts_dev, hidden_dev, width).transpose(0, 2, 1)
    up_w_grad = dot_tn(du, x_all).reshape(experts_dev, hidden_dev, width).transpose(0, 2, 1)

    select_grad = (gate_grad - jnp.sum(gate_grad * gate_own, axis=-1, keepdims=True)) / total_own
    prob_grad = mask_own * select_grad
    logit_grad = (
        prob_own * (prob_grad - jnp.sum(prob_grad * prob_own, axis=-1, keepdims=True))
    ).astype(BF16)
    router_part = dot_tn(ffn_own, logit_grad)
    ffn_grad = ffn_back + dot_nt(logit_grad, router_weight)
    ffn_gain_part = jnp.sum(ffn_grad * normed_two, axis=0)
    mid_grad = dy_rows[:part].astype(F32) + norm_reverse(ffn_grad * ffn_gain, normed_two, scale_two)
    mid_rows = gather_z(mid_grad.astype(BF16), n_t)

    d_attn = dot_nn(mid_rows, output_projection).astype(BF16)
    d_out = d_attn.reshape(tokens, kv, group, head_dim)
    delta = jnp.sum(d_out.astype(F32) * attn_out.astype(F32), axis=-1)
    delta = jnp.transpose(delta, (1, 2, 0))[..., None]
    v_grad = jnp.einsum("kgqs,qkgd->skd", probs_b, d_out, preferred_element_type=F32)
    p_grad = jnp.einsum("qkgd,skd->kgqs", d_out, v_rows, preferred_element_type=F32)
    s_grad = (probs * (p_grad - delta) * scale_value).astype(BF16)
    q_grad = jnp.einsum("kgqs,skd->qkgd", s_grad, k_rot, preferred_element_type=F32)
    k_grad = jnp.einsum("kgqs,qkgd->skd", s_grad, q_rot, preferred_element_type=F32)
    q_back = rope_back(q_grad.reshape(tokens, heads, head_dim), cos_rows, sin_rows)
    q_gain_part = jnp.sum(q_back * q_hat, axis=(0, 1))
    q_raw_grad = norm_reverse(q_back * query_norm_gain, q_hat, q_scale).astype(BF16)
    q_raw_grad = q_raw_grad.reshape(tokens, -1)
    k_back = rope_back(k_grad, cos_rows, sin_rows)
    k_gain_part = jnp.sum(k_back * k_hat, axis=(0, 1))
    k_raw_grad = norm_reverse(k_back * key_norm_gain, k_hat, k_scale).astype(BF16)
    k_raw_grad = k_raw_grad.reshape(tokens, -1)
    v_grad_b = v_grad.astype(BF16).reshape(tokens, -1)

    in_part = (
        dot_nt(q_raw_grad, query_weight)
        + dot_nt(k_raw_grad, key_projection)
        + dot_nt(v_grad_b, value_projection)
    ).astype(BF16)
    attn_in_grad = scatter_z(in_part, n_t)
    normed_own = normed_one[:part]
    attn_gain_part = jnp.sum(attn_in_grad * normed_own, axis=0)
    input_own = mid_grad + norm_reverse(attn_in_grad * attn_gain, normed_own, scale_one[:part])
    input_grad = roll_rows(gather_z(input_own.astype(BF16), n_t), turn)

    def weight_grad(rows_dp, columns_dp):
        return dot_tn(jnp.concatenate(rows_dp, 0), jnp.concatenate(columns_dp, 0))

    slab = width // n_dp

    def spread(rows):
        if n_dp != 8:
            return [lax.all_to_all(rows, "dp", split_axis=1, concat_axis=0, tiled=True)]
        out = []
        for r in range(n_dp):
            piece = lax.dynamic_slice_in_dim(rows, (d_index ^ r) * slab, slab, 1)
            out.append(piece if r == 0 else swap(piece, r, n_dp))
        return out

    attn_in_slab = spread(attn_in)
    mid_slab = spread(mid_rows)
    out_weight_grad = weight_grad(mid_slab, gather_dp(attn_flat, n_dp))
    qkv_grad = jnp.concatenate([q_raw_grad, k_raw_grad, v_grad_b], 1)
    qkv_w = weight_grad(attn_in_slab, gather_dp(qkv_grad, n_dp))
    q_cols = heads * head_dim
    kv_cols = kv * head_dim
    query_weight_grad = qkv_w[:, :q_cols]
    key_weight_grad = qkv_w[:, q_cols : q_cols + kv_cols]
    value_weight_grad = qkv_w[:, q_cols + kv_cols :]

    router_sum = lax.psum(
        lax.psum_scatter(router_part.astype(BF16), "dp", scatter_dimension=0, tiled=True), "tensor"
    ).astype(F32)
    gains = jnp.concatenate([attn_gain_part, ffn_gain_part, q_gain_part, k_gain_part])
    gains = lax.psum(gains, ("dp", "tensor"))

    def mine(vector):
        size = vector.shape[0] // n_dp
        return lax.dynamic_slice_in_dim(vector, d_index * size, size, 0)

    return (
        block_output,
        input_grad,
        mine(gains[:width]),
        query_weight_grad,
        key_weight_grad,
        value_weight_grad,
        mine(gains[2 * width : 2 * width + head_dim]),
        mine(gains[2 * width + head_dim :]),
        out_weight_grad,
        mine(gains[width : 2 * width]),
        router_sum,
        gate_w_grad,
        up_w_grad,
        down_grad,
    )


def solution(mesh):
    return jax.shard_map(
        local,
        mesh=mesh,
        in_specs=(
            P("dp", None),
            P("dp", None),
            P("dp", None),
            P(),
            P(None, "tensor"),
            P(None, "tensor"),
            P(None, "tensor"),
            P(),
            P(),
            P(None, "tensor"),
            P(),
            P(),
            P("dp", None, "tensor"),
            P("dp", None, "tensor"),
            P("dp", "tensor", None),
            P("dp", None),
        ),
        out_specs=(
            P("dp", None),
            P("dp", None),
            P("dp"),
            P("dp", "tensor"),
            P("dp", "tensor"),
            P("dp", "tensor"),
            P("dp"),
            P("dp"),
            P("dp", "tensor"),
            P("dp"),
            P("dp", None),
            P("dp", None, "tensor"),
            P("dp", None, "tensor"),
            P("dp", "tensor", None),
        ),
        check_vma=False,
    )
```

time: 1660 us -> 648 us (0.39)
  waiting for transfers between devices: 803 us -> 165 us
  blocking collectives: 469 us -> 58.9 us
  starting transfers between devices: 5.48 us -> 110 us
  local copies, waits for them, and re-layouts: 137 us -> 83.2 us
    reduce_scatter x7 -> x1, waiting for transfers between devices: 683 us -> 15.8 us  [local(): lax.psum_scatter(router_part.astype(BF16), 'dp', scatter_dimension=0, til...]
    all_to_all x3 -> x0, blocking collectives: 429 us -> none  [the longest x2 376 us: dispatch(): return lax.all_to_all(buffer, 'dp', split_axis=0, concat_axis=0, tiled=True)]
    ppermute x0 -> x102, waiting for transfers between devices: none -> 149 us  [the longest x70 104 us: swap(): return lax.ppermute(value, 'dp', [(i, i ^ bit) for i in range(count)])]
    ppermute x0 -> x102, starting transfers between devices: none -> 110 us  [the longest x32 56.7 us: shift(): lax.ppermute(value, 'tensor', [(i, (i + step) % count) for i in range(cou...]
    gather x4 -> x0, local copies, waits for them, and re-layouts: 89.4 us -> none  [the longest x2 65.4 us: pick_slots(): picked = jnp.take(token_rows, jnp.maximum(slot_token, 0), axis=0)]
    psum x2 -> x0, waiting for transfers between devices: 82.7 us -> none  [the longest x1 45.2 us: local(): lax.psum(attn_part.astype(jnp.bfloat16), 'tensor').astype(jnp.float32)]
    psum x1 -> x2, blocking collectives: 11.9 us -> 58.9 us  [the longest x1 39.3 us: local(): gains = lax.psum(gains, ('dp', 'tensor'))]
    unnamed x203 -> x290, local copies, waits for them, and re-layouts: 14.3 us -> 53.5 us
  transfers between devices with their start and end apart: 12 -> 103, of which waited for: 10 -> 31; matrix products, arithmetic and copies ran while one was open for 9% -> 30% of each run, Pallas kernels for 0% -> 0%
where the time goes in v1:
time: 648 us; the launch traced here: 638 us
  waiting for transfers between devices  165 us (25%)
  matrix products  139 us (21%)
  starting transfers between devices  110 us (17%)
  local copies, waits for them, and re-layouts  83.2 us (13%)
  other arithmetic  65 us (10%)
  blocking collectives  58.9 us (9%)
  between operations  16.9 us (3%)
    ppermute x70, waiting for transfers between devices, swap(): return lax.ppermute(value, 'dp', [(i, i ^ bit) for i in range(count)])  104 us
    ppermute x32, starting transfers between devices, shift(): lax.ppermute(value, 'tensor', [(i, (i + step) % count) for i in range(cou...  56.7 us
    unnamed x290, local copies, waits for them, and re-layouts  53.5 us
    ppermute x70, starting transfers between devices, swap(): return lax.ppermute(value, 'dp', [(i, i ^ bit) for i in range(count)])  53.5 us
    ppermute x32, waiting for transfers between devices, shift(): lax.ppermute(value, 'tensor', [(i, (i + step) % count) for i in range(cou...  44.8 us
    dot_general x9, matrix products, dot_nn(): lax.dot_general(a, b, (((1,), (0,)), ((), ())), preferred_element_type=F32)  42.5 us
    psum x1, blocking collectives, local(): gains = lax.psum(gains, ('dp', 'tensor'))  39.3 us
    dot_general x6, matrix products, dot_tn(): lax.dot_general(a, b, (((0,), (0,)), ((), ())), preferred_element_type=F32)  37.1 us
  transfers between devices with their start and end apart: 103, of which 31 were waited for; matrix products, arithmetic and copies ran while one was open for 30% of the time, Pallas kernels for 0%

profile of v1, /device:TPU:0, one launch (start us, length us, event | category | flops | bytes accessed | tf_op | source)
XLA Modules:
  0.0 638.1 jit_solution(17216061805389194970)
XLA Ops:
  75.1 4.1 collective-permute-done.76
  83.7 6.4 %collective-permute-done.1 = bf16[64,2048]{1,0:T(8,128)(2,1)S(1)} collective-permute-done((bf16[64,2048]{1,0:T(8,128)(2,1)S(1)}, bf16[64,2048]{1,0:T(8,128)(2,1)S(1)}, u32[]{:S(2)}, u32[]{:S(2)}) %collective-permute-start.1) | collective-permute-done | bytes 262176 | tf_op jit(solution)/shard_map/ppermute | solution.py:37
  121.8 9.1 %collective-permute-done.43 = bf16[256,2048]{1,0:T(8,128)(2,1)S(1)} collective-permute-done((bf16[256,2048]{1,0:T(8,128)(2,1)S(1)}, bf16[256,2048]{1,0:T(8,128)(2,1)S(1)}, u32[]{:S(2)}, u32[]{:S(2)}) %collective-permute-start.43) | collective-permute-done | bytes 1048608 | tf_op jit(solution)/shard_map/ppermute | solution.py:33
  144.5 25.2 %collective-permute-done.45 = bf16[128,2048]{1,0:T(8,128)(2,1)S(1)} collective-permute-done((bf16[128,2048]{1,0:T(8,128)(2,1)S(1)}, bf16[128,2048]{1,0:T(8,128)(2,1)S(1)}, u32[]{:S(2)}, u32[]{:S(2)}) %collective-permute-start.45) | collective-permute-done | bytes 524320 | tf_op jit(solution)/shard_map/ppermute | solution.py:33
  181.9 5.3 collective-permute-done.13
  189.9 9.1 %fusion.111 = f32[2048,768]{1,0:T(8,128)S(1)} fusion(bf16[2048,2048]{1,0:T(8,128)(2,1)} %constant_dynamic-update-slice_fusion.21, bf16[768,2048]{1,0:T(8,128)(2,1)S(1)} %bitcast.211), kind=kOutput, calls=%fused_computation.348 | convolution fusion | flops 6442450944 | bytes 17825792 | tf_op jit(solution)/shard_map/dot_general | solution.py:25
  204.4 8.6 %fusion.110 = f32[2048,768]{1,0:T(8,128)} fusion(bf16[2048,2048]{1,0:T(8,128)(2,1)S(1)} %constant_dynamic-update-slice_fusion, bf16[768,2048]{1,0:T(8,128)(2,1)S(1)} %bitcast.209), kind=kOutput, calls=%fused_computation.347 | convolution fusion | flops 6442450944 | bytes 17825792 | tf_op jit(solution)/shard_map/dot_general | solution.py:25
  213.0 8.6 %fusion.109 = f32[2048,768]{1,0:T(8,128)} fusion(bf16[2048,2048]{1,0:T(8,128)(2,1)S(1)} %constant_dynamic-update-slice_fusion, bf16[768,2048]{1,0:T(8,128)(2,1)S(1)} %bitcast.192), kind=kOutput, calls=%fused_computation.346 | convolution fusion | flops 6442450944 | bytes 17825792 | tf_op jit(solution)/shard_map/dot_general | solution.py:25
  221.6 7.6 %fusion.7 = bf16[2048,32]{0,1:T(8,128)(2,1)} fusion(f32[2048,768]{1,0:T(8,128)S(1)} %fusion.111, f32[2048,768]{1,0:T(8,128)S(1)} %copy-done.106, s32[768]{0:T(1024)S(1)} %fusion.79, f32[2048,768]{1,0:T(8,128)} %fusion.109), kind=kOutput, calls=%fused_computation.17 | convolution fusion | flops 613507072 | bytes 19008512 | tf_op jit(solution)/shard_map/dot_general | solution.py:244
  231.2 10.7 %multiply_convert_fusion = (bf16[2048,768]{1,0:T(8,128)(2,1)S(1)}, bf16[2048,768]{1,0:T(8,128)(2,1)S(1)}, bf16[2048,768]{1,0:T(8,128)(2,1)}) fusion(f32[2048,768]{1,0:T(8,128)} %copy-done.105, f32[2048,768]{1,0:T(8,128)} %fusion.109, f32[2048,768]{1,0:T(8,128)} %fusion.110, s32[768]{0:T(1024)S(1)} %fusion.79, f32[2048]{0:T(1024)S(1)} %fusion.76, ...), kind=kOutput, calls=%fused_computation.7 | convolution fusion | flops 631005184 | bytes 28666880 | tf_op jit(solution)/shard_map/dot_general | solution.py:231
  242.0 9.5 %fusion.112 = f32[2048,2048]{1,0:T(8,128)} fusion(bf16[2048,768]{1,0:T(8,128)(2,1)S(1)} %get-tuple-element.34, bf16[768,2048]{1,0:T(8,128)(2,1)S(1)} %bitcast.193), kind=kOutput, calls=%fused_computation.349 | convolution fusion | flops 6442450944 | bytes 23068672 | tf_op jit(solution)/shard_map/dot_general | solution.py:21
  251.5 12.6 %add_convert_fusion = bf16[2048,2048]{1,0:T(8,128)(2,1)} fusion(f32[2048,2048]{1,0:T(8,128)} %fusion.112, bf16[2048,768]{1,0:T(8,128)(2,1)S(1)} %get-tuple-element.33, bf16[768,2048]{1,0:T(8,128)(2,1)S(1)} %bitcast.210), kind=kOutput, calls=%fused_computation.2 | convolution fusion | flops 6450839552 | bytes 31457280 | tf_op jit(solution)/shard_map/dot_general | solution.py:21
  264.0 8.0 %fusion.1 = bf16[2048,2176]{1,0:T(8,128)(2,1)} fusion(bf16[2048,32]{1,0:T(8,128)(2,1)S(1)} %copy-done.26, bf16[2048,2048]{1,0:T(8,128)(2,1)} %add_convert_fusion), kind=kLoop, calls=%fused_computation.3 | loop fusion | flops 26738688 | bytes 17432576 | tf_op jit(solution)/shard_map/concatenate | solution.py:252
  272.0 4.2 fusion.94
  276.7 9.2 %convolution_convert_fusion = bf16[2048,2048]{1,0:T(8,128)(2,1)S(1)} fusion(bf16[2048,768]{1,0:T(8,128)(2,1)} %get-tuple-element.35, bf16[768,2048]{1,0:T(8,128)(2,1)S(1)} %bitcast.212), kind=kOutput, calls=%fused_computation.4 | convolution fusion | flops 6446645248 | bytes 14680064 | tf_op jit(solution)/shard_map/dot_general | solution.py:21
  288.4 10.5 %fusion.116 = f32[768,2048]{1,0:T(8,128)} fusion(bf16[2048,768]{1,0:T(8,128)(2,1)} %copy-done.109, bf16[2048,2048]{1,0:T(8,128)(2,1)S(1)} %bitcast.200), kind=kOutput, calls=%fused_computation.353 | convolution fusion | flops 6442450944 | bytes 17825792 | tf_op jit(solution)/shard_map/dot_general | solution.py:29
  310.9 8.4 %collective-permute-done.30 = bf16[128,2048]{1,0:T(8,128)(2,1)} collective-permute-done((bf16[128,2048]{1,0:T(8,128)(2,1)}, bf16[128,2048]{1,0:T(8,128)(2,1)}, u32[]{:S(2)}, u32[]{:S(2)}) %collective-permute-start.30) | collective-permute-done | bytes 524320 | tf_op jit(solution)/shard_map/ppermute | solution.py:33
  323.0 7.7 %collective-permute-done.54 = bf16[128,2176]{1,0:T(8,128)(2,1)S(1)} collective-permute-done((bf16[128,2176]{1,0:T(8,128)(2,1)S(1)}, bf16[128,2176]{1,0:T(8,128)(2,1)S(1)}, u32[]{:S(2)}, u32[]{:S(2)}) %collective-permute-start.54) | collective-permute-done | bytes 557088 | tf_op jit(solution)/shard_map/ppermute | solution.py:33
  337.4 10.7 %fusion.117 = f32[768,2048]{1,0:T(8,128)} fusion(bf16[2048,768]{1,0:T(8,128)(2,1)} %copy-done.108, bf16[2048,2048]{1,0:T(8,128)(2,1)S(1)} %bitcast.200), kind=kOutput, calls=%fused_computation.354 | convolution fusion | flops 6442450944 | bytes 17825792 | tf_op jit(solution)/shard_map/dot_general | solution.py:29
  348.1 9.2 %collective-permute-done.31 = bf16[256,2048]{1,0:T(8,128)(2,1)S(1)} collective-permute-done((bf16[256,2048]{1,0:T(8,128)(2,1)S(1)}, bf16[256,2048]{1,0:T(8,128)(2,1)S(1)}, u32[]{:S(2)}, u32[]{:S(2)}) %collective-permute-start.31) | collective-permute-done | bytes 1048608 | tf_op jit(solution)/shard_map/ppermute | solution.py:33
  359.3 20.0 %collective-permute-done.55 = bf16[256,2176]{1,0:T(8,128)(2,1)S(1)} collective-permute-done((bf16[256,2176]{1,0:T(8,128)(2,1)S(1)}, bf16[256,2176]{1,0:T(8,128)(2,1)S(1)}, u32[]{:S(2)}, u32[]{:S(2)}) %collective-permute-start.55) | collective-permute-done | bytes 1114144 | tf_op jit(solution)/shard_map/ppermute | solution.py:33
  395.1 11.0 %fusion.118 = f32[768,2048]{1,0:T(8,128)} fusion(bf16[2048,768]{1,0:T(8,128)(2,1)S(1)} %copy-done.107, bf16[2048,2048]{1,0:T(8,128)(2,1)} %constant_dynamic-update-slice_fusion.21), kind=kOutput, calls=%fused_computation.355 | convolution fusion | flops 6442450944 | bytes 17825792 | tf_op jit(solution)/shard_map/dot_general | solution.py:29
  416.8 7.9 %collective-permute-done.60 = bf16[64,2048]{1,0:T(8,128)(2,1)S(1)} collective-permute-done((bf16[64,2048]{1,0:T(8,128)(2,1)S(1)}, bf16[64,2048]{1,0:T(8,128)(2,1)S(1)}, u32[]{:S(2)}, u32[]{:S(2)}) %collective-permute-start.60) | collective-permute-done | bytes 262176 | tf_op jit(solution)/shard_map/ppermute | solution.py:37
  428.1 4.8 collective-permute-start.62
  433.6 15.8 %reduce-scatter.2.cloned.1.call-done = bf16[256,32]{0,1:T(8,128)(2,1)} async-done(((bf16[2048,32]{0,1:T(8,128)(2,1)}), bf16[256,32]{0,1:T(8,128)(2,1)}) %reduce-scatter.2.cloned.1.call-update) | async-done | bytes 16400 | tf_op jit(solution)/shard_map/reduce_scatter | solution.py:335
  449.4 19.5 %psum.15 = bf16[256,32]{0,1:T(8,128)(2,1)S(1)} all-reduce(bf16[256,32]{0,1:T(8,128)(2,1)} %reduce-scatter.2.cloned.1.call-done), channel_id=1, replica_groups=mesh['dp'=8,'tensor'=4] {'tensor'}, use_global_device_ids=true, to_apply=%region_29.31 | all-reduce | flops 8192 | bytes 32768 | tf_op jit(solution)/shard_map/psum | solution.py:334
  509.5 5.9 collective-permute-start.67
  516.8 5.0 collective-permute-done.67
  539.3 39.3 %psum.14 = f32[4352]{0:T(1024)S(1)} all-reduce(f32[4352]{0:T(1024)S(1)} %pad_maximum_fusion.24), channel_id=1, replica_groups=mesh['dp'=8,'tensor'=4] {'dp','tensor'}, use_global_device_ids=true, to_apply=%region_27.29 | all-reduce | flops 4352 | bytes 34816 | tf_op jit(solution)/shard_map/psum | solution.py:338
  583.2 10.7 %collective-permute-done.69 = bf16[64,2048]{1,0:T(8,128)(2,1)S(1)} collective-permute-done((bf16[64,2048]{1,0:T(8,128)(2,1)S(1)}, bf16[64,2048]{1,0:T(8,128)(2,1)S(1)}, u32[]{:S(2)}, u32[]{:S(2)}) %collective-permute-start.69) | collective-permute-done | bytes 262176 | tf_op jit(solution)/shard_map/ppermute | solution.py:37
  610.8 7.6 %fusion.33 = bf16[256,2048]{1,0:T(8,128)(2,1)} fusion(s32[]{:T(128)S(6)} %select_n.114, bf16[64,2048]{1,0:T(8,128)(2,1)} %get-tuple-element.107, bf16[64,2048]{1,0:T(8,128)(2,1)S(1)} %collective-permute-done.36, bf16[64,1024]{1,0:T(8,128)(2,1)S(1)} %collective-permute-done.38, bf16[64,1024]{1,0:T(8,128)(2,1)S(1)} %collective-permute-done.39, ...), kind=kLoop, calls=%fused_computation.92 | loop fusion | flops 10485760 | bytes 2097156 | tf_op jit(solution)/shard_map/jit(_roll_dynamic)/concatenate | solution.py:109
  618.6 6.5 %fusion.23 = bf16[256,2048]{1,0:T(8,128)(2,1)} fusion(s32[]{:T(128)S(6)} %select_n.114, bf16[64,2048]{1,0:T(8,128)(2,1)S(1)} %get-tuple-element.106, bf16[64,2048]{1,0:T(8,128)(2,1)S(1)} %collective-permute-done.68, bf16[64,1024]{1,0:T(8,128)(2,1)S(1)} %collective-permute-done.70, bf16[64,1024]{1,0:T(8,128)(2,1)S(1)} %collective-permute-done.71, ...), kind=kLoop, calls=%fused_computation.82 | loop fusion | flops 10485760 | bytes 2097156 | tf_op jit(solution)/shard_map/jit(_roll_dynamic)/concatenate | solution.py:109
  (648 shorter events, 282.4 us)
Async XLA Ops:
  7.2 442.2 %reduce-scatter.2.cloned.1.call-start = ((), (), s32[]{:S(2)}) async-start(), calls=%async_computation.1 | async-start | bytes 147456 | tf_op jit(solution)/shard_map/reduce_scatter | solution.py:335
  8.8 44.6 %collective-permute-start.16 = (s32[256,8]{0,1:T(8,128)S(1)}, s32[256,8]{0,1:T(8,128)S(1)}, u32[]{:S(2)}, u32[]{:S(2)}) collective-permute-start(s32[256,8]{0,1:T(8,128)S(1)} %get-tuple-element.28), channel_id=1, source_target_pairs={{0,4},{4,0},{8,12},{12,8},{16,20},{20,16},{24,28},{28,24},{1,5},{5... | collective-permute-start | bytes 24584 | tf_op jit(solution)/shard_map/ppermute | solution.py:33
  9.3 43.6 %collective-permute-start.17 = (s32[256,8]{0,1:T(8,128)S(1)}, s32[256,8]{0,1:T(8,128)S(1)}, u32[]{:S(2)}, u32[]{:S(2)}) collective-permute-start(s32[256,8]{0,1:T(8,128)S(1)} %get-tuple-element.28), channel_id=1, source_target_pairs={{0,8},{4,12},{8,0},{12,4},{16,24},{20,28},{24,16},{28,20},{1,9},{5... | collective-permute-start | bytes 24584 | tf_op jit(solution)/shard_map/ppermute | solution.py:33
  11.8 38.7 %collective-permute-start.19 = (s32[256,8]{0,1:T(8,128)S(1)}, s32[256,8]{0,1:T(8,128)S(1)}, u32[]{:S(2)}, u32[]{:S(2)}) collective-permute-start(s32[256,8]{0,1:T(8,128)S(1)} %get-tuple-element.28), channel_id=1, source_target_pairs={{0,16},{4,20},{8,24},{12,28},{16,0},{20,4},{24,8},{28,12},{1,17},{... | collective-permute-start | bytes 24584 | tf_op jit(solution)/shard_map/ppermute | solution.py:33
  31.7 68.2 %collective-permute-start.94 = (bf16[256,1024]{0,1:T(8,128)(2,1)}, bf16[256,1024]{0,1:T(8,128)(2,1)}, u32[]{:S(2)}, u32[]{:S(2)}) collective-permute-start(bf16[256,1024]{0,1:T(8,128)(2,1)} %bitcast.11), channel_id=1, source_target_pairs={{0,4},{4,0},{8,12},{12,8},{16,20},{20,16},{24,28},{28,24},{1,5},{5... | collective-permute-start | bytes 1572872 | tf_op jit(solution)/shard_map/ppermute | solution.py:33
  37.2 27.6 %collective-permute-start = (bf16[64,1024]{1,0:T(8,128)(2,1)}, bf16[64,1024]{1,0:T(8,128)(2,1)}, u32[]{:S(2)}, u32[]{:S(2)}) collective-permute-start(bf16[64,1024]{1,0:T(8,128)(2,1)} %get-tuple-element.100), channel_id=1, source_target_pairs={{0,1},{1,2},{2,3},{3,0},{4,5},{5,6},{6,7},{7,4},{8,9},{9,10},{10,1... | collective-permute-start | bytes 393224 | tf_op jit(solution)/shard_map/ppermute | solution.py:37
  96.8 34.2 %collective-permute-start.40 = (bf16[256,2048]{1,0:T(8,128)(2,1)}, bf16[256,2048]{1,0:T(8,128)(2,1)S(1)}, u32[]{:S(2)}, u32[]{:S(2)}) collective-permute-start(bf16[256,2048]{1,0:T(8,128)(2,1)} %get-tuple-element.22), channel_id=1, source_target_pairs={{0,4},{4,0},{8,12},{12,8},{16,20},{20,16},{24,28},{28,24},{1,5},{5... | collective-permute-start | bytes 3145736 | tf_op jit(solution)/shard_map/ppermute | solution.py:33
  106.4 24.5 %collective-permute-start.43 = (bf16[256,2048]{1,0:T(8,128)(2,1)S(1)}, bf16[256,2048]{1,0:T(8,128)(2,1)S(1)}, u32[]{:S(2)}, u32[]{:S(2)}) collective-permute-start(bf16[256,2048]{1,0:T(8,128)(2,1)S(1)} %copy-done.21), channel_id=1, source_target_pairs={{0,16},{4,20},{8,24},{12,28},{16,0},{20,4},{24,8},{28,12},{1,17},{... | collective-permute-start | bytes 3145736 | tf_op jit(solution)/shard_map/ppermute | solution.py:33
  111.7 23.8 %collective-permute-start.41 = (bf16[256,2048]{1,0:T(8,128)(2,1)S(1)}, bf16[256,2048]{1,0:T(8,128)(2,1)S(1)}, u32[]{:S(2)}, u32[]{:S(2)}) collective-permute-start(bf16[256,2048]{1,0:T(8,128)(2,1)S(1)} %copy-done.21), channel_id=1, source_target_pairs={{0,8},{4,12},{8,0},{12,4},{16,24},{20,28},{24,16},{28,20},{1,9},{5... | collective-permute-start | bytes 3145736 | tf_op jit(solution)/shard_map/ppermute | solution.py:33
  130.9 43.6 %collective-permute-start.8 = (bf16[256,2048]{1,0:T(8,128)(2,1)S(1)}, bf16[256,2048]{1,0:T(8,128)(2,1)S(1)}, u32[]{:S(2)}, u32[]{:S(2)}) collective-permute-start(bf16[256,2048]{1,0:T(8,128)(2,1)S(1)} %pad_maximum_fusion.2), channel_id=1, source_target_pairs={{0,4},{4,0},{8,12},{12,8},{16,20},{20,16},{24,28},{28,24},{1,5},{5... | collective-permute-start | bytes 3145736 | tf_op jit(solution)/shard_map/ppermute | solution.py:33
  135.5 37.2 %collective-permute-start.9 = (bf16[256,2048]{1,0:T(8,128)(2,1)S(1)}, bf16[256,2048]{1,0:T(8,128)(2,1)S(1)}, u32[]{:S(2)}, u32[]{:S(2)}) collective-permute-start(bf16[256,2048]{1,0:T(8,128)(2,1)S(1)} %pad_maximum_fusion.2), channel_id=1, source_target_pairs={{0,8},{4,12},{8,0},{12,4},{16,24},{20,28},{24,16},{28,20},{1,9},{5... | collective-permute-start | bytes 3145736 | tf_op jit(solution)/shard_map/ppermute | solution.py:33
  137.1 35.5 %collective-permute-start.11 = (bf16[256,2048]{1,0:T(8,128)(2,1)S(1)}, bf16[256,2048]{1,0:T(8,128)(2,1)S(1)}, u32[]{:S(2)}, u32[]{:S(2)}) collective-permute-start(bf16[256,2048]{1,0:T(8,128)(2,1)S(1)} %pad_maximum_fusion.2), channel_id=1, source_target_pairs={{0,16},{4,20},{8,24},{12,28},{16,0},{20,4},{24,8},{28,12},{1,17},{... | collective-permute-start | bytes 3145736 | tf_op jit(solution)/shard_map/ppermute | solution.py:33
  138.7 30.9 %collective-permute-start.45 = (bf16[128,2048]{1,0:T(8,128)(2,1)S(1)}, bf16[128,2048]{1,0:T(8,128)(2,1)S(1)}, u32[]{:S(2)}, u32[]{:S(2)}) collective-permute-start(bf16[128,2048]{1,0:T(8,128)(2,1)S(1)} %slice.463), channel_id=1, source_target_pairs={{0,8},{4,12},{8,0},{12,4},{16,24},{20,28},{24,16},{28,20},{1,9},{5... | collective-permute-start | bytes 1572872 | tf_op jit(solution)/shard_map/ppermute | solution.py:33
  141.2 30.8 %collective-permute-start.46 = (bf16[128,2048]{1,0:T(8,128)(2,1)S(1)}, bf16[128,2048]{1,0:T(8,128)(2,1)S(1)}, u32[]{:S(2)}, u32[]{:S(2)}) collective-permute-start(bf16[128,2048]{1,0:T(8,128)(2,1)S(1)} %slice.464), channel_id=1, source_target_pairs={{0,16},{4,20},{8,24},{12,28},{16,0},{20,4},{24,8},{28,12},{1,17},{... | collective-permute-start | bytes 1572872 | tf_op jit(solution)/shard_map/ppermute | solution.py:33
  176.4 22.6 %collective-permute-start.10 = (bf16[256,2048]{1,0:T(8,128)(2,1)S(1)}, bf16[256,2048]{1,0:T(8,128)(2,1)S(1)}, u32[]{:S(2)}, u32[]{:S(2)}) collective-permute-start(bf16[256,2048]{1,0:T(8,128)(2,1)S(1)} %collective-permute-done.9), channel_id=1, source_target_pairs={{0,4},{4,0},{8,12},{12,8},{16,20},{20,16},{24,28},{28,24},{1,5},{5... | collective-permute-start | bytes 3145736 | tf_op jit(solution)/shard_map/ppermute | solution.py:33
  276.2 28.0 %collective-permute-start.49 = (bf16[256,2176]{1,0:T(8,128)(2,1)}, bf16[256,2176]{1,0:T(8,128)(2,1)S(1)}, u32[]{:S(2)}, u32[]{:S(2)}) collective-permute-start(bf16[256,2176]{1,0:T(8,128)(2,1)} %get-tuple-element.39), channel_id=1, source_target_pairs={{0,4},{4,0},{8,12},{12,8},{16,20},{20,16},{24,28},{28,24},{1,5},{5... | collective-permute-start | bytes 3342344 | tf_op jit(solution)/shard_map/ppermute | solution.py:33
  276.7 28.1 %collective-permute-start.53 = (bf16[256,2176]{1,0:T(8,128)(2,1)}, bf16[256,2176]{1,0:T(8,128)(2,1)}, u32[]{:S(2)}, u32[]{:S(2)}) collective-permute-start(bf16[256,2176]{1,0:T(8,128)(2,1)} %get-tuple-element.37), channel_id=1, source_target_pairs={{0,4},{4,0},{8,12},{12,8},{16,20},{20,16},{24,28},{28,24},{1,5},{5... | collective-permute-start | bytes 3342344 | tf_op jit(solution)/shard_map/ppermute | solution.py:33
  299.0 60.3 %collective-permute-start.48 = (bf16[256,2176]{1,0:T(8,128)(2,1)}, bf16[256,2176]{1,0:T(8,128)(2,1)}, u32[]{:S(2)}, u32[]{:S(2)}) collective-permute-start(bf16[256,2176]{1,0:T(8,128)(2,1)} %get-tuple-element.36), channel_id=1, source_target_pairs={{0,4},{4,0},{8,12},{12,8},{16,20},{20,16},{24,28},{28,24},{1,5},{5... | collective-permute-start | bytes 3342344 | tf_op jit(solution)/shard_map/ppermute | solution.py:33
  300.4 36.3 %collective-permute-start.24 = (bf16[256,2048]{1,0:T(8,128)(2,1)}, bf16[256,2048]{1,0:T(8,128)(2,1)}, u32[]{:S(2)}, u32[]{:S(2)}) collective-permute-start(bf16[256,2048]{1,0:T(8,128)(2,1)} %get-tuple-element.43), channel_id=1, source_target_pairs={{0,4},{4,0},{8,12},{12,8},{16,20},{20,16},{24,28},{28,24},{1,5},{5... | collective-permute-start | bytes 3145736 | tf_op jit(solution)/shard_map/ppermute | solution.py:33
  309.4 21.3 %collective-permute-start.54 = (bf16[128,2176]{1,0:T(8,128)(2,1)S(1)}, bf16[128,2176]{1,0:T(8,128)(2,1)S(1)}, u32[]{:S(2)}, u32[]{:S(2)}) collective-permute-start(bf16[128,2176]{1,0:T(8,128)(2,1)S(1)} %get-tuple-element.67), channel_id=1, source_target_pairs={{0,8},{4,12},{8,0},{12,4},{16,24},{20,28},{24,16},{28,20},{1,9},{5... | collective-permute-start | bytes 1671176 | tf_op jit(solution)/shard_map/ppermute | solution.py:33
  322.3 35.0 %collective-permute-start.31 = (bf16[256,2048]{1,0:T(8,128)(2,1)S(1)}, bf16[256,2048]{1,0:T(8,128)(2,1)S(1)}, u32[]{:S(2)}, u32[]{:S(2)}) collective-permute-start(bf16[256,2048]{1,0:T(8,128)(2,1)S(1)} %pad_maximum_fusion.5), channel_id=1, source_target_pairs={{0,16},{4,20},{8,24},{12,28},{16,0},{20,4},{24,8},{28,12},{1,17},{... | collective-permute-start | bytes 3145736 | tf_op jit(solution)/shard_map/ppermute | solution.py:33
  330.7 26.7 %collective-permute-start.28 = (bf16[256,2048]{1,0:T(8,128)(2,1)S(1)}, bf16[256,2048]{1,0:T(8,128)(2,1)S(1)}, u32[]{:S(2)}, u32[]{:S(2)}) collective-permute-start(bf16[256,2048]{1,0:T(8,128)(2,1)S(1)} %pad_maximum_fusion.4), channel_id=1, source_target_pairs={{0,8},{4,12},{8,0},{12,4},{16,24},{20,28},{24,16},{28,20},{1,9},{5... | collective-permute-start | bytes 3145736 | tf_op jit(solution)/shard_map/ppermute | solution.py:33
  334.9 44.4 %collective-permute-start.55 = (bf16[256,2176]{1,0:T(8,128)(2,1)S(1)}, bf16[256,2176]{1,0:T(8,128)(2,1)S(1)}, u32[]{:S(2)}, u32[]{:S(2)}) collective-permute-start(bf16[256,2176]{1,0:T(8,128)(2,1)S(1)} %pad_maximum_fusion.1), channel_id=1, source_target_pairs={{0,16},{4,20},{8,24},{12,28},{16,0},{20,4},{24,8},{28,12},{1,17},{... | collective-permute-start | bytes 3342344 | tf_op jit(solution)/shard_map/ppermute | solution.py:33
  336.7 42.6 %collective-permute-start.52 = (bf16[256,2176]{1,0:T(8,128)(2,1)S(1)}, bf16[256,2176]{1,0:T(8,128)(2,1)S(1)}, u32[]{:S(2)}, u32[]{:S(2)}) collective-permute-start(bf16[256,2176]{1,0:T(8,128)(2,1)S(1)} %pad_maximum_fusion), channel_id=1, source_target_pairs={{0,8},{4,12},{8,0},{12,4},{16,24},{20,28},{24,16},{28,20},{1,9},{5... | collective-permute-start | bytes 3342344 | tf_op jit(solution)/shard_map/ppermute | solution.py:33
  415.8 113.6 %collective-permute-start.35 = (bf16[64,2048]{1,0:T(8,128)(2,1)}, bf16[64,2048]{1,0:T(8,128)(2,1)}, u32[]{:S(2)}, u32[]{:S(2)}) collective-permute-start(bf16[64,2048]{1,0:T(8,128)(2,1)} %pad_maximum_fusion.18), channel_id=1, source_target_pairs={{0,3},{1,0},{2,1},{3,2},{4,7},{5,4},{6,5},{7,6},{8,11},{9,8},{10,9... | collective-permute-start | bytes 786440 | tf_op jit(solution)/shard_map/ppermute | solution.py:37
  424.7 44.8 %collective-permute-start.63 = (bf16[64,1024]{1,0:T(8,128)(2,1)S(1)}, bf16[64,1024]{1,0:T(8,128)(2,1)S(1)}, u32[]{:S(2)}, u32[]{:S(2)}) collective-permute-start(bf16[64,1024]{1,0:T(8,128)(2,1)S(1)} %slice.490), channel_id=1, source_target_pairs={{0,3},{1,0},{2,1},{3,2},{4,7},{5,4},{6,5},{7,6},{8,11},{9,8},{10,9... | collective-permute-start | bytes 393224 | tf_op jit(solution)/shard_map/ppermute | solution.py:37
  428.1 41.4 %collective-permute-start.62 = (bf16[64,1024]{1,0:T(8,128)(2,1)S(1)}, bf16[64,1024]{1,0:T(8,128)(2,1)S(1)}, u32[]{:S(2)}, u32[]{:S(2)}) collective-permute-start(bf16[64,1024]{1,0:T(8,128)(2,1)S(1)} %slice.489), channel_id=1, source_target_pairs={{0,1},{1,2},{2,3},{3,0},{4,5},{5,6},{6,7},{7,4},{8,9},{9,10},{10,1... | collective-permute-start | bytes 393224 | tf_op jit(solution)/shard_map/ppermute | solution.py:37
  516.7 87.3 %collective-permute-start.79 = (bf16[256,1280]{1,0:T(8,128)(2,1)}, bf16[256,1280]{1,0:T(8,128)(2,1)}, u32[]{:S(2)}, u32[]{:S(2)}) collective-permute-start(bf16[256,1280]{1,0:T(8,128)(2,1)} %get-tuple-element.104), channel_id=1, source_target_pairs={{0,4},{4,0},{8,12},{12,8},{16,20},{20,16},{24,28},{28,24},{1,5},{5... | collective-permute-start | bytes 1966088 | tf_op jit(solution)/shard_map/ppermute | solution.py:33
  521.8 77.1 %collective-permute-start.80 = (bf16[256,1280]{1,0:T(8,128)(2,1)}, bf16[256,1280]{1,0:T(8,128)(2,1)}, u32[]{:S(2)}, u32[]{:S(2)}) collective-permute-start(bf16[256,1280]{1,0:T(8,128)(2,1)} %get-tuple-element.104), channel_id=1, source_target_pairs={{0,8},{4,12},{8,0},{12,4},{16,24},{20,28},{24,16},{28,20},{1,9},{5... | collective-permute-start | bytes 1966088 | tf_op jit(solution)/shard_map/ppermute | solution.py:33
  527.4 70.4 %collective-permute-start.82 = (bf16[256,1280]{1,0:T(8,128)(2,1)}, bf16[256,1280]{1,0:T(8,128)(2,1)}, u32[]{:S(2)}, u32[]{:S(2)}) collective-permute-start(bf16[256,1280]{1,0:T(8,128)(2,1)} %get-tuple-element.104), channel_id=1, source_target_pairs={{0,16},{4,20},{8,24},{12,28},{16,0},{20,4},{24,8},{28,12},{1,17},{... | collective-permute-start | bytes 1966088 | tf_op jit(solution)/shard_map/ppermute | solution.py:33
  534.3 44.3 %collective-permute-start.36 = (bf16[64,2048]{1,0:T(8,128)(2,1)}, bf16[64,2048]{1,0:T(8,128)(2,1)S(1)}, u32[]{:S(2)}, u32[]{:S(2)}) collective-permute-start(bf16[64,2048]{1,0:T(8,128)(2,1)} %get-tuple-element.107), channel_id=1, source_target_pairs={{0,3},{1,0},{2,1},{3,2},{4,7},{5,4},{6,5},{7,6},{8,11},{9,8},{10,9... | collective-permute-start | bytes 786440 | tf_op jit(solution)/shard_map/ppermute | solution.py:37
  537.0 43.2 %collective-permute-start.37 = (bf16[64,2048]{1,0:T(8,128)(2,1)}, bf16[64,2048]{1,0:T(8,128)(2,1)S(1)}, u32[]{:S(2)}, u32[]{:S(2)}) collective-permute-start(bf16[64,2048]{1,0:T(8,128)(2,1)} %get-tuple-element.107), channel_id=1, source_target_pairs={{0,1},{1,2},{2,3},{3,0},{4,5},{5,6},{6,7},{7,4},{8,9},{9,10},{10,1... | collective-permute-start | bytes 786440 | tf_op jit(solution)/shard_map/ppermute | solution.py:37
  (189 other events, 2418.6 us)
Sparse Core Ops, SparseCore 0:
  416.9 32.4 reduce-scatter.1

commit v2 on v1

v2 whole, which is shorter than its diff:
```python
import functools

import jax
import jax.numpy as jnp
from jax import lax
from jax.experimental import pallas as pl
from jax.experimental.pallas import tpu as pltpu
from jax.sharding import PartitionSpec as P

EPS = 1e-06
THETA = 1000000.0
F32 = jnp.float32
BF16 = jnp.bfloat16
LANES = 128


def rms_scale(values):
    return lax.rsqrt(jnp.mean(values * values, axis=-1, keepdims=True) + EPS)


def norm_reverse(grad_rows, normed, scale_rows):
    return scale_rows * (grad_rows - normed * jnp.mean(grad_rows * normed, axis=-1, keepdims=True))


def dot_nn(a, b):
    return lax.dot_general(a, b, (((1,), (0,)), ((), ())), preferred_element_type=F32)


def dot_nt(a, b):
    return lax.dot_general(a, b, (((1,), (1,)), ((), ())), preferred_element_type=F32)


def dot_tn(a, b):
    return lax.dot_general(a, b, (((0,), (0,)), ((), ())), preferred_element_type=F32)


def swap(value, bit, count):
    return lax.ppermute(value, "dp", [(i, i ^ bit) for i in range(count)])


def shift(value, step, count):
    return lax.ppermute(value, "tensor", [(i, (i + step) % count) for i in range(count)])


def after(value, *first):
    return lax.optimization_barrier((value,) + first)[0]


def add_b(a, b):
    return (a.astype(F32) + b.astype(F32)).astype(BF16)


def gather_eight(shard):
    half = shard.shape[0] // 16 * 8
    along_x = swap(shard, 2, 8)
    along_y = swap(shard, 4, 8)
    mate = swap(shard, 1, 8)
    diag_lo = swap(along_y[:half], 2, 8)
    diag_hi = swap(along_x[half:], 4, 8)
    mate_x = swap(along_x, 1, 8)
    mate_y = swap(along_y, 1, 8)
    diag = jnp.concatenate([diag_lo, diag_hi], 0)
    mate_d = swap(diag, 1, 8)
    return [shard, mate, along_x, mate_x, along_y, mate_y, diag, mate_d]


def scatter_eight(chunks, *first):
    mates = {r: swap(chunks[r + 1], 1, 8) for r in (0, 2, 4, 6)}
    sent = {r: swap(add_b(chunks[r], mates[r]), r, 8) for r in (2, 4, 6)}
    sent = after(sent, *first)
    total = chunks[0].astype(F32) + mates[0].astype(F32)
    for r in (2, 4, 6):
        total = total + sent[r].astype(F32)
    return total.astype(BF16)


def row_block(rows, index, count):
    size = rows.shape[0] // count
    return lax.dynamic_slice_in_dim(rows, (index % count) * size, size, 0)


def scatter_z(rows, index, count):
    if count != 4:
        return lax.psum_scatter(rows, "tensor", scatter_dimension=0, tiled=True).astype(F32)
    half = rows.shape[1] // 2
    far = row_block(rows, index + 2, count)
    lo = shift(far[:, :half], 1, count)
    hi = shift(far[:, half:], -1, count)
    zero = jnp.zeros_like(lo)
    up = add_b(row_block(rows, index + 1, count), jnp.concatenate([lo, zero], 1))
    down = add_b(row_block(rows, index + 3, count), jnp.concatenate([zero, hi], 1))
    got_up = shift(up, 1, count)
    got_down = shift(down, -1, count)
    own = row_block(rows, index, count).astype(F32)
    return own + got_up.astype(F32) + got_down.astype(F32)


def join_kernel(place, own, nxt, prev, far_lo, far_hi, out):
    size, width = own.shape
    half = width // 2
    t = place[0]

    def rows(step):
        return pl.ds(pl.multiple_of(lax.rem(t + step, 4) * size, size), size)

    out[rows(0), :] = own[...]
    out[rows(1), :] = nxt[...]
    out[rows(2), :half] = far_lo[...]
    out[rows(2), half:] = far_hi[...]
    out[rows(3), :] = prev[...]


def gather_z(shard, index, count):
    if count != 4:
        return lax.all_gather(shard, "tensor", axis=0, tiled=True)
    size, width = shard.shape
    half = width // 2
    prev = shift(shard, 1, count)
    nxt = shift(shard, -1, count)
    far_lo = shift(prev[:, :half], 1, count)
    far_hi = shift(nxt[:, half:], -1, count)
    vmem = pl.BlockSpec(memory_space=pltpu.VMEM)
    return pl.pallas_call(
        join_kernel,
        in_specs=[pl.BlockSpec(memory_space=pltpu.SMEM)] + [vmem] * 5,
        out_specs=vmem,
        out_shape=jax.ShapeDtypeStruct((count * size, width), shard.dtype),
        name="join_rows",
    )(index.reshape(1), shard, nxt, prev, far_lo, far_hi)


def split_dot(a, b, form):
    high = a.astype(BF16)
    low = (a - high.astype(F32)).astype(BF16)
    return form(high, b) + form(low, b)


def stage_kernel(count, xa, xb, dh_ref, ma, mb, wr, wg, wu, place, back_a, back_b, hg, dg, du):
    rows, width = xa.shape
    x = jnp.concatenate([xa[...], xb[...]], 0)
    logits = dot_nt(x, wr[...])
    lane = lax.broadcasted_iota(jnp.int32, logits.shape, 1)
    logits = jnp.where(lane < count, logits, -1e30)
    raised = jnp.exp(logits - jnp.max(logits, axis=-1, keepdims=True))
    chosen = raised * jnp.concatenate([ma[...], mb[...]], 0).astype(F32)
    gate = chosen / jnp.sum(chosen, axis=-1, keepdims=True)
    wide = split_dot(gate, place[...], dot_nn)
    g = dot_nt(x, wg[...])
    u = dot_nt(x, wu[...])
    dh = dh_ref[...].astype(F32)
    sig = jax.nn.sigmoid(g)
    act = g * sig
    hidden = act * u
    hg[...] = (hidden * wide).astype(BF16)
    grads = split_dot(hidden * dh, place[...], dot_nt)
    scaled = dh * wide
    dg_b = (scaled * u * sig * (1.0 + g * (1.0 - sig))).astype(BF16)
    du_b = (scaled * act).astype(BF16)
    dg[...] = dg_b
    du[...] = du_b
    back = (dot_nn(dg_b, wg[...]) + dot_nn(du_b, wu[...])).astype(BF16)
    back_a[:, :width] = back[:rows]
    back_b[:, :width] = back[rows:]
    back_a[:, width:] = grads[:rows].astype(BF16)
    back_b[:, width:] = grads[rows:].astype(BF16)


def expert_stage(xa, xb, dh, ma, mb, wr, wg, wu, place, count):
    rows, width = xa.shape
    flat = wg.shape[0]
    wide = jax.ShapeDtypeStruct((rows, width + LANES), BF16)
    tall = jax.ShapeDtypeStruct((2 * rows, flat), BF16)
    whole = lambda a: pl.BlockSpec(a.shape, lambda i: (0, 0))
    mask = pl.BlockSpec((rows, LANES), lambda i: (0, width // LANES))
    return pl.pallas_call(
        functools.partial(stage_kernel, count),
        grid=(1,),
        in_specs=[whole(xa), whole(xb), whole(dh), mask, mask, whole(wr), whole(wg), whole(wu), whole(place)],
        out_specs=[whole(a) for a in (wide, wide, tall, tall, tall)],
        out_shape=[wide, wide, tall, tall, tall],
        cost_estimate=pl.CostEstimate(
            flops=16 * rows * flat * width,
            transcendentals=2 * rows * flat,
            bytes_accessed=4 * (4 * rows * width + 2 * flat * width),
        ),
        name="expert_stage",
    )(xa, xb, dh, ma, mb, wr, wg, wu, place)


def hidden_kernel(ya, yb, wd, dh):
    rows = ya.shape[0]
    width = wd.shape[1]
    dh[:rows] = dot_nt(ya[:, :width], wd[...]).astype(BF16)
    dh[rows:] = dot_nt(yb[:, :width], wd[...]).astype(BF16)


def hidden_back(ya, yb, wd):
    rows = ya.shape[0]
    flat, width = wd.shape
    vmem = pl.BlockSpec(memory_space=pltpu.VMEM)
    return pl.pallas_call(
        hidden_kernel,
        in_specs=[vmem] * 3,
        out_specs=vmem,
        out_shape=jax.ShapeDtypeStruct((2 * rows, flat), BF16),
        cost_estimate=pl.CostEstimate(
            flops=4 * rows * flat * width,
            transcendentals=0,
            bytes_accessed=4 * rows * width + 2 * flat * width,
        ),
        name="hidden_back",
    )(ya, yb, wd)


def mix_kernel(hg, wd, mix_a, mix_b):
    rows = mix_a.shape[0]
    mix = dot_nn(hg[...], wd[...]).astype(BF16)
    mix_a[...] = mix[:rows]
    mix_b[...] = mix[rows:]


def mix_rows(hg, wd):
    rows, flat = hg.shape
    width = wd.shape[1]
    half = jax.ShapeDtypeStruct((rows // 2, width), BF16)
    vmem = pl.BlockSpec(memory_space=pltpu.VMEM)
    return pl.pallas_call(
        mix_kernel,
        in_specs=[vmem] * 2,
        out_specs=[vmem] * 2,
        out_shape=[half, half],
        cost_estimate=pl.CostEstimate(
            flops=2 * rows * flat * width,
            transcendentals=0,
            bytes_accessed=2 * rows * width + 2 * flat * width,
        ),
        name="mix_rows",
    )(hg, wd)


def weight_kernel(n_rows, n_left, *refs):
    right = refs[:n_rows]
    left = refs[n_rows : n_rows + n_left]
    outs = refs[n_rows + n_left :]
    per = n_left // len(outs)
    rows = right[0].shape[0]
    for o, out in enumerate(outs):
        total = None
        for s in range(per):
            lhs = left[o * per + s]
            for h in range(2):
                term = dot_tn(lhs[h * rows : (h + 1) * rows, :], right[2 * s + h][...])
                total = term if total is None else total + term
        out[...] = total


def weight_grads(rows_list, left_lists, width):
    rows = rows_list[0].shape[0]
    flat = left_lists[0][0].shape[1]
    block = 512
    lefts = [a for group in left_lists for a in group]
    n = len(rows_list)
    return pl.pallas_call(
        functools.partial(weight_kernel, n, len(lefts)),
        grid=(width // block,),
        in_specs=[pl.BlockSpec((rows, block), lambda j: (0, j))] * n
        + [pl.BlockSpec(a.shape, lambda j: (0, 0)) for a in lefts],
        out_specs=[pl.BlockSpec((flat, block), lambda j: (0, j))] * len(left_lists),
        out_shape=[jax.ShapeDtypeStruct((flat, width), F32)] * len(left_lists),
        cost_estimate=pl.CostEstimate(
            flops=2 * n * rows * flat * width * len(left_lists),
            transcendentals=0,
            bytes_accessed=4 * flat * width * len(left_lists) + 2 * n * rows * width,
        ),
        name="weight_grads",
    )(*rows_list, *lefts)


def tail_kernel(q_cols, kv_cols, *refs):
    slabs, qkv, ffn, attn = refs[1:9], refs[9:17], refs[17:25], refs[25:33]
    q_out, k_out, v_out, o_out, r_out, gain_out = refs[33:]
    rows = ffn[0].shape[0]
    slab = slabs[0].shape[1] // 2
    main = router = out = gains = None
    for r in range(8):
        attn_in = slabs[r][:, :slab]
        mid = slabs[r][:, slab:]
        a = dot_tn(attn_in, qkv[r][:rows, : q_cols + 2 * kv_cols])
        b = dot_tn(ffn[r][...], qkv[r][:rows, q_cols + 2 * kv_cols :])
        c = dot_tn(mid, attn[r][...])
        d = qkv[r][rows:, :].astype(F32)
        main, router, out, gains = (
            (a, b, c, d) if r == 0 else (main + a, router + b, out + c, gains + d)
        )
    q_out[...] = main[:, :q_cols]
    k_out[...] = main[:, q_cols : q_cols + kv_cols]
    v_out[...] = main[:, q_cols + kv_cols :]
    o_out[...] = out
    r_out[...] = router
    gain_out[...] = gains


def tail_grads(d_index, slabs, qkv, ffn, attn_all, q_cols, kv_cols):
    slab = slabs[0].shape[1] // 2
    rows = ffn[0].shape[0]
    cols = qkv[0].shape[1]
    extra = qkv[0].shape[0] - rows
    whole = lambda shape: pl.BlockSpec(shape, lambda i, s: (0, 0))
    outs = [(slab, q_cols), (slab, kv_cols), (slab, kv_cols), (slab, q_cols), (slab, LANES)]
    outs.append((extra, cols))
    return pl.pallas_call(
        functools.partial(tail_kernel, q_cols, kv_cols),
        grid_spec=pltpu.PrefetchScalarGridSpec(
            num_scalar_prefetch=1,
            grid=(1,),
            in_specs=[whole(a.shape) for a in slabs]
            + [whole(a.shape) for a in qkv]
            + [pl.BlockSpec((rows, slab), lambda i, s: (0, s[0])) for _ in ffn]
            + [
                pl.BlockSpec((rows, q_cols), functools.partial(lambda r, i, s: (s[0] ^ r, 0), r))
                for r in range(8)
            ],
            out_specs=[whole(shape) for shape in outs],
        ),
        out_shape=[jax.ShapeDtypeStruct(shape, F32) for shape in outs],
        name="tail_grads",
    )(d_index.reshape(1), *slabs, *qkv, *ffn, *([attn_all] * 8))


def experts_eight(ffn_rows, hidden, masks, wr, wg, wu, place, count):
    x = gather_eight(ffn_rows)
    back, hg, dg, du = [], [], [], []
    for s in range(4):
        a, b, h, g, u = expert_stage(
            x[2 * s], x[2 * s + 1], hidden[s], masks[2 * s], masks[2 * s + 1], wr, wg, wu, place, count
        )
        back += [a, b]
        hg.append(h)
        dg.append(g)
        du.append(u)
    return x, back, hg, dg, du


def rope_apply(values, cos_rows, sin_rows):
    half = values.shape[-1] // 2
    low, high = values[..., :half], values[..., half:]
    c, s = cos_rows[:, None, :], sin_rows[:, None, :]
    return jnp.concatenate([low * c - high * s, high * c + low * s], axis=-1)


def rope_back(values, cos_rows, sin_rows):
    half = values.shape[-1] // 2
    low, high = values[..., :half], values[..., half:]
    c, s = cos_rows[:, None, :], sin_rows[:, None, :]
    return jnp.concatenate([low * c + high * s, high * c - low * s], axis=-1)


def local(
    block_input,
    segment_ids,
    expert_ids,
    attn_gain,
    query_weight,
    key_projection,
    value_projection,
    query_norm_gain,
    key_norm_gain,
    output_projection,
    ffn_gain,
    router_weight,
    gate_experts,
    up_experts,
    down_experts,
    out_grad,
):
    tokens, width = block_input.shape
    head_dim = query_norm_gain.shape[0]
    experts_dev, _, hidden_dev = gate_experts.shape
    n_dp = lax.axis_size("dp")
    n_t = lax.axis_size("tensor")
    num_experts = experts_dev * n_dp
    part = tokens // n_t
    flat = experts_dev * hidden_dev
    slab = width // n_dp
    t_index = lax.axis_index("tensor")
    d_index = lax.axis_index("dp")
    scale_value = head_dim ** (-0.5)
    eight = n_dp == 8
    names = jnp.arange(num_experts, dtype=jnp.int32)
    wg = jnp.transpose(gate_experts, (0, 2, 1)).reshape(flat, width)
    wu = jnp.transpose(up_experts, (0, 2, 1)).reshape(flat, width)
    wd = down_experts.reshape(flat, width)

    seg = segment_ids[0]
    order = jnp.arange(tokens, dtype=jnp.int32)
    inputs_f = block_input.astype(F32)
    scale_one = rms_scale(inputs_f)
    normed_one = inputs_f * scale_one
    attn_in = (normed_one * attn_gain).astype(BF16)
    same = seg[:, None] == seg[None, :]
    positions = jnp.sum((same & (order[None, :] < order[:, None])).astype(jnp.int32), axis=1)
    frequency = THETA ** (-(jnp.arange(head_dim // 2, dtype=F32) * 2.0) / head_dim)
    angles = positions.astype(F32)[:, None] * frequency[None, :]
    cos_rows, sin_rows = jnp.cos(angles), jnp.sin(angles)
    allowed = same & (order[None, :] <= order[:, None])
    q_raw = dot_nn(attn_in, query_weight).reshape(tokens, -1, head_dim)
    q_scale = rms_scale(q_raw)
    q_hat = q_raw * q_scale
    k_raw = dot_nn(attn_in, key_projection).reshape(tokens, -1, head_dim)
    k_scale = rms_scale(k_raw)
    k_hat = k_raw * k_scale
    k_rot = rope_apply(k_hat * key_norm_gain, cos_rows, sin_rows).astype(BF16)
    v_rows = dot_nn(attn_in, value_projection).astype(BF16).reshape(tokens, -1, head_dim)
    heads = q_raw.shape[1]
    kv = k_raw.shape[1]
    group = heads // kv
    q_cols = heads * head_dim
    kv_cols = kv * head_dim
    q_rot = rope_apply(q_hat * query_norm_gain, cos_rows, sin_rows).astype(BF16)
    q_rot = q_rot.reshape(tokens, kv, group, head_dim)
    scores = jnp.einsum("qkgd,skd->kgqs", q_rot, k_rot, preferred_element_type=F32) * scale_value
    scores = jnp.where(allowed, scores, -jnp.inf)
    top = jnp.max(scores, axis=-1, keepdims=True)
    weights = jnp.exp(scores - top)
    totals = jnp.sum(weights, axis=-1, keepdims=True)
    probs = weights / totals
    probs_b = probs.astype(BF16)
    attn_out = jnp.einsum("kgqs,skd->qkgd", probs_b, v_rows, preferred_element_type=F32)
    attn_out = attn_out.astype(BF16)
    attn_flat = attn_out.reshape(tokens, q_cols)
    attn_part = dot_nt(attn_flat, output_projection).astype(BF16)
    attn_sum = lax.psum(attn_part, "tensor").astype(F32)

    pad = -num_experts % LANES
    mask_own = jnp.any(expert_ids[:, :, None] == names[None, None, :], axis=1).astype(F32)
    owner = d_index * experts_dev + jnp.arange(flat, dtype=jnp.int32) // hidden_dev
    place = (names[:, None] == owner[None, :]).astype(BF16)
    place = jnp.pad(place, ((0, pad), (0, 0)))
    wr = jnp.pad(router_weight.T, ((0, pad), (0, 0)))
    dy_wide = jnp.concatenate([out_grad, jnp.pad(mask_own, ((0, 0), (0, pad))).astype(BF16)], 1)
    dy_wide = after(dy_wide, attn_part)
    if eight:
        dy_chunks = gather_eight(dy_wide)
        hidden = [hidden_back(dy_chunks[2 * s], dy_chunks[2 * s + 1], wd) for s in range(4)]
        attn_sum = after(attn_sum, dy_chunks[6], hidden[:3], place, wr)
    else:
        dy_all = lax.all_gather(dy_wide, "dp", axis=0, tiled=True)
        mask_all = dy_all[:, width : width + num_experts].astype(F32)
        dy_all = dy_all[:, :width]

    middle = inputs_f + attn_sum
    scale_two = rms_scale(middle)
    normed_two = middle * scale_two
    ffn_rows = (normed_two * ffn_gain).astype(BF16)
    logits = dot_nn(ffn_rows, router_weight)
    raised = jnp.exp(logits - jnp.max(logits, axis=-1, keepdims=True))
    prob = raised / jnp.sum(raised, axis=-1, keepdims=True)
    selected = prob * mask_own
    total_own = jnp.sum(selected, axis=-1, keepdims=True)
    gate_own = selected / total_own

    if eight:
        x_chunks, back, hg, dg, du = experts_eight(
            ffn_rows, hidden, dy_chunks, wr, wg, wu, place, num_experts
        )
        mix = [m for s in range(4) for m in mix_rows(hg[s], wd)]
        back_sum = scatter_eight(back, mix)
    else:
        x_all = lax.all_gather(ffn_rows, "dp", axis=0, tiled=True)
        lg = dot_nt(x_all, wr)[:, :num_experts]
        chosen = jnp.exp(lg - jnp.max(lg, axis=-1, keepdims=True)) * mask_all
        gate_all = chosen / jnp.sum(chosen, axis=-1, keepdims=True)
        spots = place[:num_experts].astype(F32)
        wide = jnp.dot(gate_all, spots, precision=lax.Precision.HIGHEST)
        d_hidden = dot_nt(dy_all, wd)
        gate_pre = dot_nt(x_all, wg)
        up_pre = dot_nt(x_all, wu)
        sig = jax.nn.sigmoid(gate_pre)
        act = gate_pre * sig
        hidden = act * up_pre
        hg_all = (hidden * wide).astype(BF16)
        grads = jnp.dot(hidden * d_hidden, spots.T, precision=lax.Precision.HIGHEST)
        scaled = d_hidden * wide
        dg_all = (scaled * up_pre * sig * (1.0 + gate_pre * (1.0 - sig))).astype(BF16)
        du_all = (scaled * act).astype(BF16)
        back = (dot_nn(dg_all, wg) + dot_nn(du_all, wu)).astype(BF16)
        back = jnp.concatenate([back, jnp.pad(grads, ((0, 0), (0, pad))).astype(BF16)], 1)
        back_sum = lax.psum_scatter(back, "dp", scatter_dimension=0, tiled=True)
    back_own = lax.psum(back_sum, "tensor").astype(F32)

    if eight:
        mix_sum = scatter_eight([after(m, back_sum) for m in mix])
        (down_grad,) = weight_grads(dy_chunks, [hg], width)
        gate_grad_w, up_grad_w = weight_grads(x_chunks, [dg, du], width)
        back_own = after(back_own, mix_sum, down_grad, gate_grad_w, up_grad_w)
    else:
        mix = dot_nn(hg_all, wd).astype(BF16)
        mix_sum = lax.psum_scatter(mix, "dp", scatter_dimension=0, tiled=True)
        down_grad = dot_tn(hg_all, dy_all)
        gate_grad_w = dot_tn(dg_all, x_all)
        up_grad_w = dot_tn(du_all, x_all)
    mine = (jnp.arange(tokens, dtype=jnp.int32) // part == t_index)[:, None]
    mix_sum = (mix_sum.astype(F32) + jnp.where(mine, middle, 0.0)).astype(BF16)
    down_grad = down_grad.reshape(experts_dev, hidden_dev, width)
    gate_grad_w = gate_grad_w.reshape(experts_dev, hidden_dev, width).transpose(0, 2, 1)
    up_grad_w = up_grad_w.reshape(experts_dev, hidden_dev, width).transpose(0, 2, 1)

    ffn_back = back_own[:, :width]
    gate_grad = back_own[:, width : width + num_experts]
    select_grad = (gate_grad - jnp.sum(gate_grad * gate_own, axis=-1, keepdims=True)) / total_own
    prob_grad = mask_own * select_grad
    logit_grad = (
        prob * (prob_grad - jnp.sum(prob_grad * prob, axis=-1, keepdims=True))
    ).astype(BF16)
    ffn_grad = ffn_back + dot_nt(logit_grad, router_weight)
    ffn_gain_part = jnp.sum(ffn_grad * normed_two, axis=0)
    mid_grad = out_grad.astype(F32) + norm_reverse(ffn_grad * ffn_gain, normed_two, scale_two)
    mid_rows = mid_grad.astype(BF16)
    block_output = lax.psum(after(mix_sum, mid_rows), "tensor")

    d_attn = dot_nn(mid_rows, output_projection).astype(BF16)
    d_out = d_attn.reshape(tokens, kv, group, head_dim)
    delta = jnp.sum(d_out.astype(F32) * attn_out.astype(F32), axis=-1)
    delta = jnp.transpose(delta, (1, 2, 0))[..., None]
    v_grad = jnp.einsum("kgqs,qkgd->skd", probs_b, d_out, preferred_element_type=F32)
    p_grad = jnp.einsum("qkgd,skd->kgqs", d_out, v_rows, preferred_element_type=F32)
    s_grad = (probs * (p_grad - delta) * scale_value).astype(BF16)
    q_grad = jnp.einsum("kgqs,skd->qkgd", s_grad, k_rot, preferred_element_type=F32)
    k_grad = jnp.einsum("kgqs,qkgd->skd", s_grad, q_rot, preferred_element_type=F32)
    q_back = rope_back(q_grad.reshape(tokens, heads, head_dim), cos_rows, sin_rows)
    q_gain_part = jnp.sum(q_back * q_hat, axis=(0, 1))
    q_raw_grad = norm_reverse(q_back * query_norm_gain, q_hat, q_scale).astype(BF16)
    q_raw_grad = q_raw_grad.reshape(tokens, -1)
    k_back = rope_back(k_grad, cos_rows, sin_rows)
    k_gain_part = jnp.sum(k_back * k_hat, axis=(0, 1))
    k_raw_grad = norm_reverse(k_back * key_norm_gain, k_hat, k_scale).astype(BF16)
    k_raw_grad = k_raw_grad.reshape(tokens, -1)
    v_grad_b = v_grad.astype(BF16).reshape(tokens, -1)

    in_f = (
        dot_nt(q_raw_grad, query_weight)
        + dot_nt(k_raw_grad, key_projection)
        + dot_nt(v_grad_b, value_projection)
    )
    in_part = in_f.astype(BF16)
    attn_in_grad = scatter_z(in_part, t_index, n_t)
    normed_own = row_block(normed_one, t_index, n_t)
    scale_own = row_block(scale_one, t_index, n_t)
    mid_own = row_block(mid_grad, t_index, n_t)
    input_own = mid_own + norm_reverse(attn_in_grad * attn_gain, normed_own, scale_own)
    input_grad = gather_z(input_own.astype(BF16), t_index, n_t)
    block_output = after(block_output, input_own)

    attn_gain_part = jnp.sum(in_f * normed_one, axis=0)
    extra = 8
    cols = q_cols + 2 * kv_cols + num_experts + pad
    gains = jnp.concatenate([attn_gain_part, ffn_gain_part / n_t, q_gain_part, k_gain_part])
    gains = jnp.pad(gains, (0, extra * cols - gains.shape[0])).reshape(extra, cols).astype(BF16)
    logit_pad = jnp.pad(logit_grad, ((0, 0), (0, pad)))
    qkv = jnp.concatenate([q_raw_grad, k_raw_grad, v_grad_b, logit_pad], 1)
    if eight:
        qkv = jnp.concatenate([qkv, gains], 0)
        qkv_chunks = gather_eight(qkv)
        attn_late = after(attn_flat, q_raw_grad)
        attn_all = lax.all_gather(attn_late, "dp", axis=0, tiled=True)
        slabs = []
        sent_in, sent_mid = lax.optimization_barrier((attn_in, mid_rows, in_part))[:2]
        for r in range(8):
            start = (d_index ^ r) * slab
            piece = jnp.concatenate(
                [lax.dynamic_slice_in_dim(a, start, slab, 1) for a in (sent_in, sent_mid)], 1
            )
            slabs.append(piece if r == 0 else swap(piece, r, 8))
        q_w, k_w, v_w, out_w, router_w, gain_sum = tail_grads(
            d_index, slabs, qkv_chunks, x_chunks, attn_all, q_cols, kv_cols
        )
        router_w = router_w[:, :num_experts]
    else:
        spread = lambda a: lax.all_to_all(a, "dp", split_axis=1, concat_axis=0, tiled=True)
        attn_all = lax.all_gather(attn_flat, "dp", axis=0, tiled=True)
        qkv_all = lax.all_gather(qkv, "dp", axis=0, tiled=True)
        qkv_w = dot_tn(spread(attn_in), qkv_all)
        q_w = qkv_w[:, :q_cols]
        k_w = qkv_w[:, q_cols : q_cols + kv_cols]
        v_w = qkv_w[:, q_cols + kv_cols : q_cols + 2 * kv_cols]
        out_w = dot_tn(spread(mid_rows), attn_all)
        x_slab = lax.dynamic_slice_in_dim(x_all, d_index * slab, slab, 1)
        router_w = dot_tn(x_slab, qkv_all[:, q_cols + 2 * kv_cols :])[:, :num_experts]
        gain_sum = lax.psum(gains.astype(F32), "dp")
    gain_flat = gain_sum.reshape(-1)

    def piece_of(start, length):
        size = length // n_dp
        return lax.dynamic_slice_in_dim(gain_flat, start + d_index * size, size, 0)

    spans = [(0, width), (width, width), (2 * width, head_dim), (2 * width + head_dim, head_dim)]
    packed = jnp.concatenate([piece_of(a, b) for a, b in spans])
    packed = jnp.pad(packed, (0, -packed.shape[0] % 1024)).reshape(-1, LANES)
    if n_t == 4:
        packed = packed + lax.ppermute(packed, "tensor", [(i, i ^ 1) for i in range(4)])
        packed = packed + lax.ppermute(packed, "tensor", [(i, i ^ 2) for i in range(4)])
    else:
        packed = lax.psum(packed, "tensor")
    packed = packed.reshape(-1)
    sizes = [b // n_dp for _, b in spans]
    starts = [sum(sizes[:i]) for i in range(4)]
    attn_gain_grad, ffn_gain_grad, q_gain_grad, k_gain_grad = [
        packed[s : s + n] for s, n in zip(starts, sizes)
    ]
    return (
        block_output,
        input_grad,
        attn_gain_grad,
        q_w,
        k_w,
        v_w,
        q_gain_grad,
        k_gain_grad,
        out_w,
        ffn_gain_grad,
        router_w,
        gate_grad_w,
        up_grad_w,
        down_grad,
    )


def solution(mesh):
    return jax.shard_map(
        local,
        mesh=mesh,
        in_specs=(
            P("dp", None),
            P("dp", None),
            P("dp", None),
            P(),
            P(None, "tensor"),
            P(None, "tensor"),
            P(None, "tensor"),
            P(),
            P(),
            P(None, "tensor"),
            P(),
            P(),
            P("dp", None, "tensor"),
            P("dp", None, "tensor"),
            P("dp", "tensor", None),
            P("dp", None),
        ),
        out_specs=(
            P("dp", None),
            P("dp", None),
            P("dp"),
            P("dp", "tensor"),
            P("dp", "tensor"),
            P("dp", "tensor"),
            P("dp"),
            P("dp"),
            P("dp", "tensor"),
            P("dp"),
            P("dp", None),
            P("dp", None, "tensor"),
            P("dp", None, "tensor"),
            P("dp", "tensor", None),
        ),
        check_vma=False,
    )
```

time: 648 us -> 508 us (0.78)
  Pallas kernels: 0 us -> 142 us
  matrix products: 139 us -> 20.4 us
  blocking collectives: 58.9 us -> 0 us
  starting transfers between devices: 110 us -> 56.2 us
  local copies, waits for them, and re-layouts: 83.2 us -> 42.1 us
    pallas_call x0 -> x16, Pallas kernels: none -> 142 us  [the longest x4 57.6 us: expert_stage(): pl.pallas_call(functools.partial(stage_kernel, count), grid=(1,), in_spec...]
    psum x2 -> x0, blocking collectives: 58.9 us -> none  [the longest x1 39.3 us: local(): gains = lax.psum(gains, ('dp', 'tensor'))]
    dot_general x8 -> x0, matrix products: 55.4 us -> none  [the longest x6 37.1 us: dot_tn(): lax.dot_general(a, b, (((0,), (0,)), ((), ())), preferred_element_type=F32)]
    ppermute x32 -> x8, starting transfers between devices: 56.7 us -> 12.1 us  [shift(): lax.ppermute(value, 'tensor', [(i, (i + step) % count) for i in range(cou...]
    psum x0 -> x3, waiting for transfers between devices: none -> 43.1 us  [the longest x1 22.5 us: local(): back_own = lax.psum(back_sum, 'tensor').astype(F32)]
    dot_general x9 -> x5, matrix products: 42.5 us -> 6.01 us  [dot_nn(): lax.dot_general(a, b, (((1,), (0,)), ((), ())), preferred_element_type=F32)]
    unnamed x290 -> x194, local copies, waits for them, and re-layouts: 53.5 us -> 19.3 us
    dot_general x8 -> x5, matrix products: 34.8 us -> 8.59 us  [dot_nt(): lax.dot_general(a, b, (((1,), (1,)), ((), ())), preferred_element_type=F32)]
  transfers between devices with their start and end apart: 103 -> 59, of which waited for: 31 -> 17; matrix products, arithmetic and copies ran while one was open for 30% -> 13% of each run, Pallas kernels for 0% -> 27%
where the time goes in v2:
time: 508 us; the launch traced here: 500 us
  waiting for transfers between devices  162 us (32%)
  Pallas kernels  142 us (28%)
  other arithmetic  63 us (12%)
  starting transfers between devices  56.2 us (11%)
  local copies, waits for them, and re-layouts  42.1 us (8%)
  matrix products  20.4 us (4%)
  between operations  15.7 us (3%)
    ppermute x45, waiting for transfers between devices, swap(): return lax.ppermute(value, 'dp', [(i, i ^ bit) for i in range(count)])  92.3 us
    pallas_call x4, Pallas kernels, expert_stage(): pl.pallas_call(functools.partial(stage_kernel, count), grid=(1,), in_spec...  57.6 us
    ppermute x45, starting transfers between devices, swap(): return lax.ppermute(value, 'dp', [(i, i ^ bit) for i in range(count)])  43.8 us
    pallas_call x2, Pallas kernels, weight_grads(): pl.pallas_call(functools.partial(weight_kernel, n, len(lefts)), grid=(wid...  30.4 us
    ppermute x8, waiting for transfers between devices, shift(): lax.ppermute(value, 'tensor', [(i, (i + step) % count) for i in range(cou...  26 us
    psum x1, waiting for transfers between devices, local(): back_own = lax.psum(back_sum, 'tensor').astype(F32)  22.5 us
    pallas_call x4, Pallas kernels, hidden_back(): pl.pallas_call(hidden_kernel, in_specs=[vmem] * 3, out_specs=vmem, out_sh...  21.5 us
    pallas_call x4, Pallas kernels, mix_rows(): pl.pallas_call(mix_kernel, in_specs=[vmem] * 2, out_specs=[vmem] * 2, out...  20.8 us
  transfers between devices with their start and end apart: 59, of which 17 were waited for; matrix products, arithmetic and copies ran while one was open for 13% of the time, Pallas kernels for 27%

profile of v2, /device:TPU:0, one launch (start us, length us, event | category | flops | bytes accessed | tf_op | source)
XLA Modules:
  0.0 500.4 jit_solution(17835737193189093117)
XLA Ops:
  32.1 22.8 %collective-permute-done.ya.ma.refs_4_ = bf16[256,2176]{1,0:T(8,128)(2,1)S(1)} collective-permute-done((bf16[256,2176]{1,0:T(8,128)(2,1)S(1)}, bf16[256,2176]{1,0:T(8,128)(2,1)S(1)}, u32[]{:S(2)}, u32[]{:S(2)}) %collective-permute-start) | collective-permute-done | bytes 1114144 | tf_op jit(solution)/shard_map/ppermute | solution.py:38
  62.8 20.6 %all-reduce.12.cloned.1.call-done = bf16[256,2048]{1,0:T(8,128)(2,1)} async-done(((bf16[256,2048]{1,0:T(8,128)(2,1)}), bf16[256,2048]{1,0:T(8,128)(2,1)}) %all-reduce.12.cloned.1.call-update) | async-done | bytes 1048592 | tf_op jit(solution)/shard_map/psum | solution.py:432
  86.2 5.3 %hidden_back.4.dh_ref = bf16[512,768]{1,0:T(8,128)(2,1)} custom-call(bf16[256,2176]{1,0:T(8,128)(2,1)} %copy-done.16, bf16[256,2176]{1,0:T(8,128)(2,1)} %collective-permute-done.4.yb.mb.refs_1_, bf16[768,2048]{1,0:T(8,128)(2,1)} %bitcast.184), custom_call_target="tpu_custom_call" | custom-call | flops 1610612736 | bytes 5242880 | tf_op jit(solution)/shard_map/hidden_back/pallas_call | solution.py:201
  93.7 5.7 %hidden_back.5.dh_ref = bf16[512,768]{1,0:T(8,128)(2,1)} custom-call(bf16[256,2176]{1,0:T(8,128)(2,1)} %collective-permute-done.2.ya.ma.refs_2_, bf16[256,2176]{1,0:T(8,128)(2,1)} %collective-permute-done.5.yb.mb.refs_3_, bf16[768,2048]{1,0:T(8,128)(2,1)} %bitcast.185), custom_call_target="tpu_custom_call" | custom-call | flops 1610612736 | bytes 5242880 | tf_op jit(solution)/shard_map/hidden_back/pallas_call | solution.py:201
  99.4 5.3 %hidden_back.6.dh_ref = bf16[512,768]{1,0:T(8,128)(2,1)} custom-call(bf16[256,2176]{1,0:T(8,128)(2,1)} %copy-done.25, bf16[256,2176]{1,0:T(8,128)(2,1)} %collective-permute-done.6.yb.mb.refs_5_, bf16[768,2048]{1,0:T(8,128)(2,1)} %bitcast.186), custom_call_target="tpu_custom_call" | custom-call | flops 1610612736 | bytes 5242880 | tf_op jit(solution)/shard_map/hidden_back/pallas_call | solution.py:201
  111.1 22.4 %collective-permute-done.9.xa.refs_2_.refs_19_ = bf16[256,2048]{1,0:T(8,128)(2,1)} collective-permute-done((bf16[256,2048]{1,0:T(8,128)(2,1)}, bf16[256,2048]{1,0:T(8,128)(2,1)}, u32[]{:S(2)}, u32[]{:S(2)}) %collective-permute-start.9) | collective-permute-done | bytes 1048608 | tf_op jit(solution)/shard_map/ppermute | solution.py:38
  140.3 5.3 %hidden_back.7.dh_ref = bf16[512,768]{1,0:T(8,128)(2,1)} custom-call(bf16[256,2176]{1,0:T(8,128)(2,1)} %copy-done.26, bf16[256,2176]{1,0:T(8,128)(2,1)} %collective-permute-done.20.yb.mb.refs_7_, bf16[768,2048]{1,0:T(8,128)(2,1)} %bitcast.187), custom_call_target="tpu_custom_call" | custom-call | flops 1610612736 | bytes 5242880 | tf_op jit(solution)/shard_map/hidden_back/pallas_call | solution.py:201
  146.1 3.9 collective-permute-done.17
  154.9 14.7 %expert_stage.5 = (bf16[256,2176]{1,0:T(8,128)(2,1)}, bf16[256,2176]{1,0:T(8,128)(2,1)}, bf16[512,768]{1,0:T(8,128)(2,1)}, bf16[512,768]{1,0:T(8,128)(2,1)}, bf16[512,768]{1,0:T(8,128)(2,1)}) custom-call(bf16[256,2048]{1,0:T(8,128)(2,1)} %collective-permute-done.9.xa.refs_2_.refs_19_, bf16[256,2048]{1,0:T(8,128)(2,1)} %collective-permute-done.10.xb.refs_3_.refs_20_, ...), custom_call_target="tpu_custom_call" | custom-call | flops 6442450944 | bytes 20971520 | tf_op jit(solution)/shard_map/expert_stage/pallas_call | solution.py:175
  170.1 14.1 %expert_stage.6 = (bf16[256,2176]{1,0:T(8,128)(2,1)}, bf16[256,2176]{1,0:T(8,128)(2,1)}, bf16[512,768]{1,0:T(8,128)(2,1)}, bf16[512,768]{1,0:T(8,128)(2,1)}, bf16[512,768]{1,0:T(8,128)(2,1)}) custom-call(bf16[256,2048]{1,0:T(8,128)(2,1)} %copy-done.28, bf16[256,2048]{1,0:T(8,128)(2,1)} %collective-permute-done.14.xb.refs_5_.refs_22_, ...), custom_call_target="tpu_custom_call" | custom-call | flops 6442450944 | bytes 20971520 | tf_op jit(solution)/shard_map/expert_stage/pallas_call | solution.py:175
  184.2 14.6 %expert_stage.7 = (bf16[256,2176]{1,0:T(8,128)(2,1)}, bf16[256,2176]{1,0:T(8,128)(2,1)}, bf16[512,768]{1,0:T(8,128)(2,1)}, bf16[512,768]{1,0:T(8,128)(2,1)}, bf16[512,768]{1,0:T(8,128)(2,1)}) custom-call(bf16[256,2048]{1,0:T(8,128)(2,1)} %constant_dynamic-update-slice_fusion.2.xa.refs_6_.refs_23_, ...), custom_call_target="tpu_custom_call" | custom-call | flops 6442450944 | bytes 20971520 | tf_op jit(solution)/shard_map/expert_stage/pallas_call | solution.py:175
  209.4 14.3 %expert_stage.4 = (bf16[256,2176]{1,0:T(8,128)(2,1)}, bf16[256,2176]{1,0:T(8,128)(2,1)}, bf16[512,768]{1,0:T(8,128)(2,1)}, bf16[512,768]{1,0:T(8,128)(2,1)}, bf16[512,768]{1,0:T(8,128)(2,1)}) custom-call(bf16[256,2048]{1,0:T(8,128)(2,1)} %multiply_convert_fusion.xa.refs_0_.refs_17_, bf16[256,2048]{1,0:T(8,128)(2,1)} %collective-permute-done.7.xb.refs_1_.refs_18_, ...), custom_call_target="tpu_custom_call" | custom-call | flops 6442450944 | bytes 20971520 | tf_op jit(solution)/shard_map/expert_stage/pallas_call | solution.py:175
  226.1 5.2 %mix_rows.4 = (bf16[256,2048]{1,0:T(8,128)(2,1)}, bf16[256,2048]{1,0:T(8,128)(2,1)}) custom-call(bf16[512,768]{1,0:T(8,128)(2,1)} %get-tuple-element.74.hg.refs_8_, bf16[768,2048]{1,0:T(8,128)(2,1)} %bitcast.188), custom_call_target="tpu_custom_call" | custom-call | flops 1610612736 | bytes 5242880 | tf_op jit(solution)/shard_map/mix_rows/pallas_call | solution.py:227
  231.3 5.2 %mix_rows.5 = (bf16[256,2048]{1,0:T(8,128)(2,1)}, bf16[256,2048]{1,0:T(8,128)(2,1)}) custom-call(bf16[512,768]{1,0:T(8,128)(2,1)} %get-tuple-element.85.hg.refs_9_, bf16[768,2048]{1,0:T(8,128)(2,1)} %bitcast.189), custom_call_target="tpu_custom_call" | custom-call | flops 1610612736 | bytes 5242880 | tf_op jit(solution)/shard_map/mix_rows/pallas_call | solution.py:227
  236.5 5.2 %mix_rows.6 = (bf16[256,2048]{1,0:T(8,128)(2,1)}, bf16[256,2048]{1,0:T(8,128)(2,1)}) custom-call(bf16[512,768]{1,0:T(8,128)(2,1)} %get-tuple-element.88.hg.refs_10_, bf16[768,2048]{1,0:T(8,128)(2,1)} %bitcast.190), custom_call_target="tpu_custom_call" | custom-call | flops 1610612736 | bytes 5242880 | tf_op jit(solution)/shard_map/mix_rows/pallas_call | solution.py:227
  241.7 5.2 %mix_rows.7 = (bf16[256,2048]{1,0:T(8,128)(2,1)}, bf16[256,2048]{1,0:T(8,128)(2,1)}) custom-call(bf16[512,768]{1,0:T(8,128)(2,1)} %get-tuple-element.91.hg.refs_11_, bf16[768,2048]{1,0:T(8,128)(2,1)} %bitcast.191), custom_call_target="tpu_custom_call" | custom-call | flops 1610612736 | bytes 5242880 | tf_op jit(solution)/shard_map/mix_rows/pallas_call | solution.py:227
  246.8 8.9 %collective-permute-done.16 = bf16[256,2176]{1,0:T(8,128)(2,1)} collective-permute-done((bf16[256,2176]{1,0:T(8,128)(2,1)}, bf16[256,2176]{1,0:T(8,128)(2,1)}, u32[]{:S(2)}, u32[]{:S(2)}) %collective-permute-start.16) | collective-permute-done | bytes 1114144 | tf_op jit(solution)/shard_map/ppermute | solution.py:38
  255.8 4.3 add_convert_fusion
  262.9 11.4 %weight_grads.2 = f32[768,2048]{1,0:T(8,128)} custom-call(bf16[256,2176]{1,0:T(8,128)(2,1)} %copy-done.16, bf16[256,2176]{1,0:T(8,128)(2,1)} %collective-permute-done.4.yb.mb.refs_1_, bf16[256,2176]{1,0:T(8,128)(2,1)} %collective-permute-done.2.ya.ma.refs_2_, bf16[256,2176]{1,0:T(8,128)(2,1)} %collective-permute-done.5.yb.mb.refs_3_, ...), custom_call_target="tpu_custom_call" | custom-call | flops 6442450944 | bytes 14680064 | tf_op jit(solution)/shard_map/weight_grads/pallas_call | solution.py:263
  286.5 19.0 %weight_grads.3 = (f32[768,2048]{1,0:T(8,128)}, f32[768,2048]{1,0:T(8,128)}) custom-call(bf16[256,2048]{1,0:T(8,128)(2,1)} %multiply_convert_fusion.xa.refs_0_.refs_17_, bf16[256,2048]{1,0:T(8,128)(2,1)} %collective-permute-done.7.xb.refs_1_.refs_18_, bf16[256,2048]{1,0:T(8,128)(2,1)} %collective-permute-done.9.xa.refs_2_.refs_19_, ...), custom_call_target="tpu_custom_call" | custom-call | flops 12884901888 | bytes 20971520 | tf_op jit(solution)/shard_map/weight_grads/pallas_call | solution.py:263
  305.6 22.5 %all-reduce.14.cloned.1.call-done = bf16[256,2176]{1,0:T(8,128)(2,1)} async-done(((bf16[256,2176]{1,0:T(8,128)(2,1)}), bf16[256,2176]{1,0:T(8,128)(2,1)}) %all-reduce.14.cloned.1.call-update) | async-done | bytes 1114128 | tf_op jit(solution)/shard_map/psum | solution.py:489
  330.9 4.3 add_convert_fusion.4
  385.6 16.7 %collective-permute-done.48.refs_13_ = bf16[264,1408]{1,0:T(8,128)(2,1)} collective-permute-done((bf16[264,1408]{1,0:T(8,128)(2,1)S(1)}, bf16[264,1408]{1,0:T(8,128)(2,1)}, u32[]{:S(2)}, u32[]{:S(2)}) %collective-permute-start.48) | collective-permute-done | bytes 743456 | tf_op jit(solution)/shard_map/ppermute | solution.py:38
  410.4 8.0 %collective-permute-done.39.refs_3_ = bf16[256,512]{1,0:T(8,128)(2,1)S(1)} collective-permute-done((bf16[256,512]{1,0:T(8,128)(2,1)S(1)}, bf16[256,512]{1,0:T(8,128)(2,1)S(1)}, u32[]{:S(2)}, u32[]{:S(2)}) %collective-permute-start.39) | collective-permute-done | bytes 262176 | tf_op jit(solution)/shard_map/ppermute | solution.py:38
  425.9 7.0 %collective-permute-start.47 = (bf16[264,1408]{1,0:T(8,128)(2,1)}, bf16[264,1408]{1,0:T(8,128)(2,1)}, u32[]{:S(2)}, u32[]{:S(2)}) collective-permute-start(bf16[264,1408]{1,0:T(8,128)(2,1)} %collective-permute-done.46.refs_11_), channel_id=1, source_target_pairs={{0,4},{4,0},{8,12},{12,8},{16,20},{20,16},{24,28},{28,24},{1,5},{5... | collective-permute-start | bytes 2230280 | tf_op jit(solution)/shard_map/ppermute | solution.py:38
  432.9 3.5 collective-permute-done.33
  437.2 6.0 %collective-permute-done.31 = bf16[64,2048]{1,0:T(8,128)(2,1)S(1)} collective-permute-done((bf16[64,2048]{1,0:T(8,128)(2,1)S(1)}, bf16[64,2048]{1,0:T(8,128)(2,1)S(1)}, u32[]{:S(2)}, u32[]{:S(2)}) %collective-permute-start.31) | collective-permute-done | bytes 262176 | tf_op jit(solution)/shard_map/ppermute | solution.py:42
  447.4 5.1 %collective-permute-done.44.refs_8_ = bf16[256,512]{1,0:T(8,128)(2,1)S(1)} collective-permute-done((bf16[256,512]{1,0:T(8,128)(2,1)S(1)}, bf16[256,512]{1,0:T(8,128)(2,1)S(1)}, u32[]{:S(2)}, u32[]{:S(2)}) %collective-permute-start.44) | collective-permute-done | bytes 262176 | tf_op jit(solution)/shard_map/ppermute | solution.py:38
  455.6 9.1 %tail_grads.1 = (f32[256,1024]{1,0:T(8,128)}, f32[256,128]{1,0:T(8,128)}, f32[256,128]{1,0:T(8,128)}, f32[256,1024]{1,0:T(8,128)}, f32[256,128]{1,0:T(8,128)}, /*index=5*/f32[8,1408]{1,0:T(8,128)}) custom-call(s32[1]{0:T(128)} %bitcast.47.refs_0_, bf16[256,512]{1,0:T(8,128)(2,1)} %pad_maximum_fusion.3.refs_1_, ...), custom_call_target="tpu_custom_call" | custom-call | tf_op jit(solution)/shard_map/tail_grads/pallas_call | solution.py:311
  465.7 11.9 %collective-permute-done.35.prev = bf16[64,2048]{1,0:T(8,128)(2,1)S(1)} collective-permute-done((bf16[64,2048]{1,0:T(8,128)(2,1)S(1)}, bf16[64,2048]{1,0:T(8,128)(2,1)S(1)}, u32[]{:S(2)}, u32[]{:S(2)}) %collective-permute-start.35) | collective-permute-done | bytes 262176 | tf_op jit(solution)/shard_map/ppermute | solution.py:42
  478.3 3.3 collective-permute-start.37
  481.7 4.2 collective-permute-done.36.far_lo
  (420 shorter events, 170.1 us)
Async XLA Ops:
  7.2 76.2 %all-reduce.12.cloned.1.call-start = ((), (), s32[]{:S(2)}) async-start(), calls=%async_computation | async-start | bytes 2097152 | tf_op jit(solution)/shard_map/psum | solution.py:432
  27.3 27.6 %collective-permute-start = (bf16[256,2176]{1,0:T(8,128)(2,1)S(1)}, bf16[256,2176]{1,0:T(8,128)(2,1)S(1)}, u32[]{:S(2)}, u32[]{:S(2)}) collective-permute-start(bf16[256,2176]{1,0:T(8,128)(2,1)S(1)} %pad_maximum_fusion.ya.ma.refs_0_), channel_id=1, source_target_pairs={{0,16},{4,20},{8,24},{12,28},{16,0},{20,4},{24,8},{28,12},{1,17},{... | collective-permute-start | bytes 3342344 | tf_op jit(solution)/shard_map/ppermute | solution.py:38
  30.3 27.2 %collective-permute-start.2 = (bf16[256,2176]{1,0:T(8,128)(2,1)S(1)}, bf16[256,2176]{1,0:T(8,128)(2,1)}, u32[]{:S(2)}, u32[]{:S(2)}) collective-permute-start(bf16[256,2176]{1,0:T(8,128)(2,1)S(1)} %pad_maximum_fusion.ya.ma.refs_0_), channel_id=1, source_target_pairs={{0,8},{4,12},{8,0},{12,4},{16,24},{20,28},{24,16},{28,20},{1,9},{5... | collective-permute-start | bytes 3342344 | tf_op jit(solution)/shard_map/ppermute | solution.py:38
  31.8 54.4 %collective-permute-start.4 = (bf16[256,2176]{1,0:T(8,128)(2,1)S(1)}, bf16[256,2176]{1,0:T(8,128)(2,1)}, u32[]{:S(2)}, u32[]{:S(2)}) collective-permute-start(bf16[256,2176]{1,0:T(8,128)(2,1)S(1)} %pad_maximum_fusion.ya.ma.refs_0_), channel_id=1, source_target_pairs={{0,4},{4,0},{8,12},{12,8},{16,20},{20,16},{24,28},{28,24},{1,5},{5... | collective-permute-start | bytes 3342344 | tf_op jit(solution)/shard_map/ppermute | solution.py:38
  31.9 296.2 %all-reduce.14.cloned.1.call-start = ((), (), s32[]{:S(2)}) async-start(), calls=%async_computation.1 | async-start | bytes 2228224 | tf_op jit(solution)/shard_map/psum | solution.py:489
  55.8 35.7 %collective-permute-start.1 = (bf16[128,2176]{1,0:T(8,128)(2,1)}, bf16[128,2176]{1,0:T(8,128)(2,1)}, u32[]{:S(2)}, u32[]{:S(2)}) collective-permute-start(bf16[128,2176]{1,0:T(8,128)(2,1)} %slice.112), channel_id=1, source_target_pairs={{0,8},{4,12},{8,0},{12,4},{16,24},{20,28},{24,16},{28,20},{1,9},{5... | collective-permute-start | bytes 1671176 | tf_op jit(solution)/shard_map/ppermute | solution.py:38
  57.5 36.2 %collective-permute-start.5 = (bf16[256,2176]{1,0:T(8,128)(2,1)}, bf16[256,2176]{1,0:T(8,128)(2,1)}, u32[]{:S(2)}, u32[]{:S(2)}) collective-permute-start(bf16[256,2176]{1,0:T(8,128)(2,1)} %collective-permute-done.2.ya.ma.refs_2_), channel_id=1, source_target_pairs={{0,4},{4,0},{8,12},{12,8},{16,20},{20,16},{24,28},{28,24},{1,5},{5... | collective-permute-start | bytes 3342344 | tf_op jit(solution)/shard_map/ppermute | solution.py:38
  59.5 33.1 %collective-permute-start.3 = (bf16[128,2176]{1,0:T(8,128)(2,1)}, bf16[128,2176]{1,0:T(8,128)(2,1)}, u32[]{:S(2)}, u32[]{:S(2)}) collective-permute-start(bf16[128,2176]{1,0:T(8,128)(2,1)} %slice.113), channel_id=1, source_target_pairs={{0,16},{4,20},{8,24},{12,28},{16,0},{20,4},{24,8},{28,12},{1,17},{... | collective-permute-start | bytes 1671176 | tf_op jit(solution)/shard_map/ppermute | solution.py:38
  61.1 38.3 %collective-permute-start.6 = (bf16[256,2176]{1,0:T(8,128)(2,1)S(1)}, bf16[256,2176]{1,0:T(8,128)(2,1)}, u32[]{:S(2)}, u32[]{:S(2)}) collective-permute-start(bf16[256,2176]{1,0:T(8,128)(2,1)S(1)} %collective-permute-done.ya.ma.refs_4_), channel_id=1, source_target_pairs={{0,4},{4,0},{8,12},{12,8},{16,20},{20,16},{24,28},{28,24},{1,5},{5... | collective-permute-start | bytes 3342344 | tf_op jit(solution)/shard_map/ppermute | solution.py:38
  108.2 25.3 %collective-permute-start.9 = (bf16[256,2048]{1,0:T(8,128)(2,1)}, bf16[256,2048]{1,0:T(8,128)(2,1)}, u32[]{:S(2)}, u32[]{:S(2)}) collective-permute-start(bf16[256,2048]{1,0:T(8,128)(2,1)} %multiply_convert_fusion.xa.refs_0_.refs_17_), channel_id=1, source_target_pairs={{0,8},{4,12},{8,0},{12,4},{16,24},{20,28},{24,16},{28,20},{1,9},{5... | collective-permute-start | bytes 3145736 | tf_op jit(solution)/shard_map/ppermute | solution.py:38
  111.1 29.2 %collective-permute-start.20 = (bf16[256,2176]{1,0:T(8,128)(2,1)S(1)}, bf16[256,2176]{1,0:T(8,128)(2,1)}, u32[]{:S(2)}, u32[]{:S(2)}) collective-permute-start(bf16[256,2176]{1,0:T(8,128)(2,1)S(1)} %copy-done.27), channel_id=1, source_target_pairs={{0,4},{4,0},{8,12},{12,8},{16,20},{20,16},{24,28},{28,24},{1,5},{5... | collective-permute-start | bytes 3342344 | tf_op jit(solution)/shard_map/ppermute | solution.py:38
  140.3 69.1 %collective-permute-start.7 = (bf16[256,2048]{1,0:T(8,128)(2,1)}, bf16[256,2048]{1,0:T(8,128)(2,1)}, u32[]{:S(2)}, u32[]{:S(2)}) collective-permute-start(bf16[256,2048]{1,0:T(8,128)(2,1)} %multiply_convert_fusion.xa.refs_0_.refs_17_), channel_id=1, source_target_pairs={{0,4},{4,0},{8,12},{12,8},{16,20},{20,16},{24,28},{28,24},{1,5},{5... | collective-permute-start | bytes 3145736 | tf_op jit(solution)/shard_map/ppermute | solution.py:38
  154.9 29.3 %collective-permute-start.19 = (bf16[256,2048]{1,0:T(8,128)(2,1)}, bf16[256,2048]{1,0:T(8,128)(2,1)}, u32[]{:S(2)}, u32[]{:S(2)}) collective-permute-start(bf16[256,2048]{1,0:T(8,128)(2,1)} %constant_dynamic-update-slice_fusion.2.xa.refs_6_.refs_23_), channel_id=1, source_target_pairs={{0,4},{4,0},{8,12},{12,8},{16,20},{20,16},{24,28},{28,24},{1,5},{5... | collective-permute-start | bytes 3145736 | tf_op jit(solution)/shard_map/ppermute | solution.py:38
  169.6 29.7 %collective-permute-start.11 = (bf16[256,2176]{1,0:T(8,128)(2,1)}, bf16[256,2176]{1,0:T(8,128)(2,1)}, u32[]{:S(2)}, u32[]{:S(2)}) collective-permute-start(bf16[256,2176]{1,0:T(8,128)(2,1)} %get-tuple-element.79), channel_id=1, source_target_pairs={{0,4},{4,0},{8,12},{12,8},{16,20},{20,16},{24,28},{28,24},{1,5},{5... | collective-permute-start | bytes 3342344 | tf_op jit(solution)/shard_map/ppermute | solution.py:38
  202.1 44.7 %collective-permute-start.12 = (bf16[256,2176]{1,0:T(8,128)(2,1)}, bf16[256,2176]{1,0:T(8,128)(2,1)}, u32[]{:S(2)}, u32[]{:S(2)}) collective-permute-start(bf16[256,2176]{1,0:T(8,128)(2,1)} %add_convert_fusion.3), channel_id=1, source_target_pairs={{0,8},{4,12},{8,0},{12,4},{16,24},{20,28},{24,16},{28,20},{1,9},{5... | collective-permute-start | bytes 3342344 | tf_op jit(solution)/shard_map/ppermute | solution.py:38
  205.2 50.5 %collective-permute-start.16 = (bf16[256,2176]{1,0:T(8,128)(2,1)}, bf16[256,2176]{1,0:T(8,128)(2,1)}, u32[]{:S(2)}, u32[]{:S(2)}) collective-permute-start(bf16[256,2176]{1,0:T(8,128)(2,1)} %add_convert_fusion.2), channel_id=1, source_target_pairs={{0,16},{4,20},{8,24},{12,28},{16,0},{20,4},{24,8},{28,12},{1,17},{... | collective-permute-start | bytes 3342344 | tf_op jit(solution)/shard_map/ppermute | solution.py:38
  208.0 47.8 %collective-permute-start.22 = (bf16[256,2176]{1,0:T(8,128)(2,1)}, bf16[256,2176]{1,0:T(8,128)(2,1)}, u32[]{:S(2)}, u32[]{:S(2)}) collective-permute-start(bf16[256,2176]{1,0:T(8,128)(2,1)} %add_convert_fusion.1), channel_id=1, source_target_pairs={{0,24},{4,28},{8,16},{12,20},{16,8},{20,12},{24,0},{28,4},{1,25},{... | collective-permute-start | bytes 3342344 | tf_op jit(solution)/shard_map/ppermute | solution.py:38
  223.7 32.1 %collective-permute-start.8 = (bf16[256,2176]{1,0:T(8,128)(2,1)}, bf16[256,2176]{1,0:T(8,128)(2,1)}, u32[]{:S(2)}, u32[]{:S(2)}) collective-permute-start(bf16[256,2176]{1,0:T(8,128)(2,1)} %get-tuple-element.77), channel_id=1, source_target_pairs={{0,4},{4,0},{8,12},{12,8},{16,20},{20,16},{24,28},{28,24},{1,5},{5... | collective-permute-start | bytes 3342344 | tf_op jit(solution)/shard_map/ppermute | solution.py:38
  274.2 56.7 %collective-permute-start.23 = (bf16[256,2048]{1,0:T(8,128)(2,1)}, bf16[256,2048]{1,0:T(8,128)(2,1)}, u32[]{:S(2)}, u32[]{:S(2)}) collective-permute-start(bf16[256,2048]{1,0:T(8,128)(2,1)} %get-tuple-element.98), channel_id=1, source_target_pairs={{0,4},{4,0},{8,12},{12,8},{16,20},{20,16},{24,28},{28,24},{1,5},{5... | collective-permute-start | bytes 3145736 | tf_op jit(solution)/shard_map/ppermute | solution.py:38
  274.8 180.8 %all-gather.2.cloned.1.call-start = ((), (), s32[]{:S(2)}) async-start(), calls=%async_computation.3 | async-start | bytes 4718592 | tf_op jit(solution)/shard_map/all_gather | solution.py:565
  277.8 53.1 %collective-permute-start.25 = (bf16[256,2048]{1,0:T(8,128)(2,1)}, bf16[256,2048]{1,0:T(8,128)(2,1)}, u32[]{:S(2)}, u32[]{:S(2)}) collective-permute-start(bf16[256,2048]{1,0:T(8,128)(2,1)} %add_convert_fusion.8), channel_id=1, source_target_pairs={{0,8},{4,12},{8,0},{12,4},{16,24},{20,28},{24,16},{28,20},{1,9},{5... | collective-permute-start | bytes 3145736 | tf_op jit(solution)/shard_map/ppermute | solution.py:38
  281.9 49.0 %collective-permute-start.27 = (bf16[256,2048]{1,0:T(8,128)(2,1)}, bf16[256,2048]{1,0:T(8,128)(2,1)}, u32[]{:S(2)}, u32[]{:S(2)}) collective-permute-start(bf16[256,2048]{1,0:T(8,128)(2,1)} %add_convert_fusion.7), channel_id=1, source_target_pairs={{0,16},{4,20},{8,24},{12,28},{16,0},{20,4},{24,8},{28,12},{1,17},{... | collective-permute-start | bytes 3145736 | tf_op jit(solution)/shard_map/ppermute | solution.py:38
  286.0 44.9 %collective-permute-start.29 = (bf16[256,2048]{1,0:T(8,128)(2,1)}, bf16[256,2048]{1,0:T(8,128)(2,1)}, u32[]{:S(2)}, u32[]{:S(2)}) collective-permute-start(bf16[256,2048]{1,0:T(8,128)(2,1)} %add_convert_fusion.6), channel_id=1, source_target_pairs={{0,24},{4,28},{8,16},{12,20},{16,8},{20,12},{24,0},{28,4},{1,25},{... | collective-permute-start | bytes 3145736 | tf_op jit(solution)/shard_map/ppermute | solution.py:38
  359.0 130.2 %all-reduce.16.cloned.1.call-start = ((), (), s32[]{:S(2)}) async-start(), calls=%async_computation.2 | async-start | bytes 2097152 | tf_op jit(solution)/shard_map/psum | solution.py:519
  372.3 31.2 %collective-permute-start.46 = (bf16[264,1408]{1,0:T(8,128)(2,1)S(1)}, bf16[264,1408]{1,0:T(8,128)(2,1)}, u32[]{:S(2)}, u32[]{:S(2)}) collective-permute-start(bf16[264,1408]{1,0:T(8,128)(2,1)S(1)} %fusion.19.refs_9_), channel_id=1, source_target_pairs={{0,8},{4,12},{8,0},{12,4},{16,24},{20,28},{24,16},{28,20},{1,9},{5... | collective-permute-start | bytes 2230280 | tf_op jit(solution)/shard_map/ppermute | solution.py:38
  373.8 28.6 %collective-permute-start.48 = (bf16[264,1408]{1,0:T(8,128)(2,1)S(1)}, bf16[264,1408]{1,0:T(8,128)(2,1)}, u32[]{:S(2)}, u32[]{:S(2)}) collective-permute-start(bf16[264,1408]{1,0:T(8,128)(2,1)S(1)} %fusion.19.refs_9_), channel_id=1, source_target_pairs={{0,16},{4,20},{8,24},{12,28},{16,0},{20,4},{24,8},{28,12},{1,17},{... | collective-permute-start | bytes 2230280 | tf_op jit(solution)/shard_map/ppermute | solution.py:38
  376.0 31.1 %collective-permute-start.30 = (bf16[64,1024]{1,0:T(8,128)(2,1)}, bf16[64,1024]{1,0:T(8,128)(2,1)}, u32[]{:S(2)}, u32[]{:S(2)}) collective-permute-start(bf16[64,1024]{1,0:T(8,128)(2,1)} %get-tuple-element.239), channel_id=1, source_target_pairs={{0,1},{1,2},{2,3},{3,0},{4,5},{5,6},{6,7},{7,4},{8,9},{9,10},{10,1... | collective-permute-start | bytes 393224 | tf_op jit(solution)/shard_map/ppermute | solution.py:42
  377.4 31.8 %collective-permute-start.32 = (bf16[64,1024]{1,0:T(8,128)(2,1)}, bf16[64,1024]{1,0:T(8,128)(2,1)}, u32[]{:S(2)}, u32[]{:S(2)}) collective-permute-start(bf16[64,1024]{1,0:T(8,128)(2,1)} %get-tuple-element.240), channel_id=1, source_target_pairs={{0,3},{1,0},{2,1},{3,2},{4,7},{5,4},{6,5},{7,6},{8,11},{9,8},{10,9... | collective-permute-start | bytes 393224 | tf_op jit(solution)/shard_map/ppermute | solution.py:42
  381.8 28.5 %collective-permute-start.38 = (bf16[256,512]{1,0:T(8,128)(2,1)}, bf16[256,512]{1,0:T(8,128)(2,1)}, u32[]{:S(2)}, u32[]{:S(2)}) collective-permute-start(bf16[256,512]{1,0:T(8,128)(2,1)} %pad_maximum_fusion.4), channel_id=1, source_target_pairs={{0,4},{4,0},{8,12},{12,8},{16,20},{20,16},{24,28},{28,24},{1,5},{5... | collective-permute-start | bytes 786440 | tf_op jit(solution)/shard_map/ppermute | solution.py:38
  420.9 32.4 %collective-permute-start.45 = (bf16[264,1408]{1,0:T(8,128)(2,1)S(1)}, bf16[264,1408]{1,0:T(8,128)(2,1)S(1)}, u32[]{:S(2)}, u32[]{:S(2)}) collective-permute-start(bf16[264,1408]{1,0:T(8,128)(2,1)S(1)} %fusion.19.refs_9_), channel_id=1, source_target_pairs={{0,4},{4,0},{8,12},{12,8},{16,20},{20,16},{24,28},{28,24},{1,5},{5... | collective-permute-start | bytes 2230280 | tf_op jit(solution)/shard_map/ppermute | solution.py:38
  425.9 29.6 %collective-permute-start.47 = (bf16[264,1408]{1,0:T(8,128)(2,1)}, bf16[264,1408]{1,0:T(8,128)(2,1)}, u32[]{:S(2)}, u32[]{:S(2)}) collective-permute-start(bf16[264,1408]{1,0:T(8,128)(2,1)} %collective-permute-done.46.refs_11_), channel_id=1, source_target_pairs={{0,4},{4,0},{8,12},{12,8},{16,20},{20,16},{24,28},{28,24},{1,5},{5... | collective-permute-start | bytes 2230280 | tf_op jit(solution)/shard_map/ppermute | solution.py:38
  452.6 25.7 %collective-permute-start.34 = (bf16[64,2048]{1,0:T(8,128)(2,1)S(1)}, bf16[64,2048]{1,0:T(8,128)(2,1)S(1)}, u32[]{:S(2)}, u32[]{:S(2)}) collective-permute-start(bf16[64,2048]{1,0:T(8,128)(2,1)S(1)} %multiply_add_fusion.2.own), channel_id=1, source_target_pairs={{0,3},{1,0},{2,1},{3,2},{4,7},{5,4},{6,5},{7,6},{8,11},{9,8},{10,9... | collective-permute-start | bytes 786440 | tf_op jit(solution)/shard_map/ppermute | solution.py:42
  (120 other events, 1090.3 us)
Sparse Core Ops, SparseCore 0:
  32.0 51.3 all-reduce.11
  274.9 53.1 all-reduce.13
  359.2 45.7 all-gather.1
  407.2 71.5 all-reduce.15
